TPU v7x, 128 devices: a whole 4x4x4 slice. The times are simulated.
128 devices in a mesh: region: 4 (over x), space: 32 (over z, y, core).
Axes of the slice: x: 4, y: 4, z: 4, core: 2. Of those that a mesh axis runs over, the one named last changes fastest.
Arguments:
- features: bfloat16 [2048, 64, 512], P(('region', 'space')), may hold values from -6 to 6
- fine_weight: bfloat16 [7, 64, 64], replicated, may hold values from -0.25 to 0.25
- down_weight: bfloat16 [8, 64, 128], replicated, may hold values from -0.25 to 0.25
- coarse_weight: bfloat16 [128, 128], replicated, may hold values from -0.5 to 0.5
- cotangent: bfloat16 [1024, 512, 128], P(('region', 'space')), may hold values from -6 to 6
- face_source: int32 [2048, 6], P(('region', 'space')), may hold values from -1 to 119, as said below
- face_requests: int32 [128, 24], P(('region', 'space')), may hold values from -1 to 95, as said below
- child_slot: int32 [2048], P(('region', 'space')), may hold values from 0 to 63, as said below
- parent_octant: int32 [128, 64], P(('region', 'space')), may hold values from -1 to 63, as said below
Outputs:
- grad_in: bfloat16 [2048, 64, 512], P(('region', 'space'))
- coarse_out: bfloat16 [1024, 512, 128], P(('region', 'space'))
- grad_fine: float32 [7, 64, 64], replicated
- grad_down: float32 [8, 64, 128], replicated
- grad_coarse: float32 [128, 128], replicated
Inputs may be any that keep to these rules, and one draw needn't show every extreme that they name: `face_source`: -1 marks a face without neighbour. A code c below 96 names brick c // 6 of the same device and its face c % 6; a larger code names received slot c - 96 = k * 4 + s, slot s of what the device whose neighbour in direction k is this device sends in direction k. The face named is always the opposite face, d with its lowest bit flipped. Each used received slot is named by exactly one (brick, direction) of its receiver. face_requests[h, k * 4 + s] is brick * 6 + face of device h that h sends in slot s to its neighbour in direction k, or -1; in each (h, k) the used slots come first; slots toward a missing neighbour are -1; it agrees with face_source of the receiver; in every draw one device receives 4 faces from each of its neighbours. `child_slot`: owner * 2 + slot, owner counted within the sender's region; distinct on each device; in every region one owner receives 2 children from every device of the region. parent_octant[q, x * 2 + u] is parent * 8 + octant on device q for the child that device x of q's region sends in slot u to q, or -1 where none is sent; distinct on each device; some parents and octants receive no child.
All inputs are finite; a program needn't handle non-finite values.
Results may differ from a plain program's by a relative error of at most 0.0069.
Values may be sent and summed in bfloat16 or wider, within the bound.
A program may use at most 192 MiB of HBM per device.

v0:
```python
import functools
import math

import jax
import jax.numpy as jnp
import numpy as np
from jax import lax
from jax.experimental import pallas as pl
from jax.experimental.pallas import tpu as pltpu
from jax.sharding import PartitionSpec as P

EDGE = 8
BF = jnp.bfloat16
F32 = jnp.float32
MESH = pl.DeviceIdType.MESH
NT = (((1,), (1,)), ((), ()))
TN = (((0,), (0,)), ((), ()))
VMEM_SPEC = pl.BlockSpec(memory_space=pltpu.VMEM)
SMEM_SPEC = pl.BlockSpec(memory_space=pltpu.SMEM)
ANY_SPEC = pl.BlockSpec(memory_space=pl.ANY)
ROWS = 128
LANES = 256
CHUNK = 8


def row_of(i, j, k):
    return i * 16 + j * 4 + k


def make_tables():
    order = np.zeros((512, 512), np.float32)
    for i in range(8):
        for j in range(8):
            for k in range(8):
                q = (j % 2) * 2 + k % 2
                order[q * 128 + row_of(i, j // 2, k // 2), i * 64 + j * 8 + k] = 1
    face = np.zeros((128, 128), np.float32)
    shift = np.zeros((4, 128, 192), np.float32)
    for i in range(8):
        for m in range(4):
            face[i * 4 + m, row_of(i, 0, m)] = 1
            face[32 + i * 4 + m, row_of(i, 3, m)] = 1
            face[64 + i * 4 + m, row_of(i, m, 0)] = 1
            face[96 + i * 4 + m, row_of(i, m, 3)] = 1
            for n in range(4):
                r = row_of(i, m, n)
                shift[0, r, row_of(i, m + 1, n) if m < 3 else 128 + i * 4 + n] = 1
                shift[1, r, row_of(i, m - 1, n) if m > 0 else 128 + i * 4 + n] = 1
                shift[2, r, row_of(i, m, n + 1) if n < 3 else 160 + i * 4 + m] = 1
                shift[3, r, row_of(i, m, n - 1) if n > 0 else 160 + i * 4 + m] = 1
    back = np.zeros((4, 160, 128), np.float32)
    back[:, :128] = shift[:, :, :128]
    back[0, 128:] = face[0:32]
    back[1, 128:] = face[32:64]
    back[2, 128:] = face[64:96]
    back[3, 128:] = face[96:128]
    spread = np.zeros((2, 128, 192), np.float32)
    for half in range(2):
        j_face = face[0:32] if half == 0 else face[32:64]
        parts = [j_face, j_face, face[64:96], face[64:96], face[96:128], face[96:128]]
        spread[half] = np.concatenate(parts, axis=0).T
    cast = lambda a: np.asarray(a, dtype=BF)
    return cast(order), cast(face), cast(shift), cast(back), cast(spread)


ORDER, FACE, SHIFT, BACK, SPREAD = make_tables()


def dot(a, b, dims=(((1,), (0,)), ((), ()))):
    return lax.dot_general(a, b, dims, preferred_element_type=F32)


def first_kernel(req_ref, slot_ref, feat_ref, cot_ref, order_ref, face_ref,
                 x_ref, table_ref, out_ref, cots_ref):
    def gather_cot(s, carry):
        cots_ref[s] = cot_ref[jnp.maximum(slot_ref[0, s], 0)]
        return carry

    lax.fori_loop(0, 64, gather_cot, 0, unroll=4)

    def four(g, carry):
        block = feat_ref[pl.ds(g * 4, 4)].reshape(256, 512)
        turned = dot(order_ref[...], block, NT).astype(BF)
        for n in range(4):
            b = g * 4 + n
            x = jnp.concatenate(
                [turned[q * 128:(q + 1) * 128, n * 64:(n + 1) * 64] for q in range(4)], axis=1
            )
            x_ref[b] = x
            f = dot(face_ref[...], x).astype(BF)
            base = b * 6
            table_ref[base] = jnp.concatenate([x[0:16, 0:128], x[0:16, 128:256]], axis=0)
            table_ref[base + 1] = jnp.concatenate([x[112:128, 0:128], x[112:128, 128:256]], axis=0)
            table_ref[base + 2] = f[0:32, 0:128]
            table_ref[base + 3] = f[32:64, 128:256]
            table_ref[base + 4] = jnp.concatenate([f[64:96, 0:64], f[64:96, 128:192]], axis=1)
            table_ref[base + 5] = jnp.concatenate([f[96:128, 64:128], f[96:128, 192:256]], axis=1)
        return carry

    lax.fori_loop(0, 4, four, 0)

    def gather_face(s, carry):
        out_ref[s] = table_ref[jnp.maximum(req_ref[0, s], 0)]
        return carry

    lax.fori_loop(0, 24, gather_face, 0, unroll=4)


def neighbours(regions, owners):
    far = owners // 4
    return [(1, 0), (-1, 0), (0, 1), (0, -1), (0, far), (0, -far)]


def face_moves(regions, owners, my_r, my_s, backward):
    sign = -1 if backward else 1
    for k, (dr, ds) in enumerate(neighbours(regions, owners)):
        to_r, to_s = my_r + sign * dr, my_s + sign * ds
        from_r, from_s = my_r - sign * dr, my_s - sign * ds
        can_send = (to_r >= 0) & (to_r < regions) & (to_s >= 0) & (to_s < owners)
        can_take = (from_r >= 0) & (from_r < regions) & (from_s >= 0) & (from_s < owners)
        yield k, (to_r, to_s), can_send, can_take


def greet_region(regions, owners, my_r, my_s):
    barrier = pltpu.get_barrier_semaphore()

    def greet(step, carry):
        peer = lax.rem(my_s + step, owners)
        pl.semaphore_signal(barrier, inc=1, device_id=(my_r, peer), device_id_type=MESH)
        return carry

    lax.fori_loop(1, owners, greet, 0)

    @pl.when(my_r > 0)
    def _():
        pl.semaphore_signal(barrier, inc=1, device_id=(my_r - 1, my_s), device_id_type=MESH)

    @pl.when(my_r < regions - 1)
    def _():
        pl.semaphore_signal(barrier, inc=1, device_id=(my_r + 1, my_s), device_id_type=MESH)

    lower = jnp.where(my_r > 0, 1, 0)
    upper = jnp.where(my_r < regions - 1, 1, 0)
    pl.semaphore_wait(barrier, owners - 1 + lower + upper)


def send_faces(regions, owners, my_r, my_s, backward, src, dst, send_sem, recv_sem):
    for k, target, can_send, can_take in face_moves(regions, owners, my_r, my_s, backward):
        copy = pltpu.make_async_remote_copy(
            src_ref=src.at[k], dst_ref=dst.at[k], send_sem=send_sem.at[k],
            recv_sem=recv_sem.at[k], device_id=target, device_id_type=MESH)

        @pl.when(can_send)
        def _():
            copy.start()


def wait_faces(regions, owners, my_r, my_s, backward, src, dst, send_sem, recv_sem):
    for k, target, can_send, can_take in face_moves(regions, owners, my_r, my_s, backward):
        copy = pltpu.make_async_remote_copy(
            src_ref=src.at[k], dst_ref=dst.at[k], send_sem=send_sem.at[k],
            recv_sem=recv_sem.at[k], device_id=target, device_id_type=MESH)

        @pl.when(can_send)
        def _():
            copy.wait_send()

        @pl.when(can_take)
        def _():
            copy.wait_recv()


def start_blocks(owners, my_r, my_s, src, dst, send_sem, recv_sem):
    def start(step, carry):
        peer = lax.rem(my_s + step, owners)
        pltpu.make_async_remote_copy(
            src_ref=src.at[peer], dst_ref=dst.at[my_s], send_sem=send_sem.at[peer],
            recv_sem=recv_sem.at[my_s], device_id=(my_r, peer), device_id_type=MESH).start()
        return carry

    lax.fori_loop(1, owners, start, 0)


def wait_blocks(owners, my_r, my_s, src, dst, send_sem, recv_sem):
    def wait(step, carry):
        peer = lax.rem(my_s + step, owners)
        copy = pltpu.make_async_remote_copy(
            src_ref=src.at[peer], dst_ref=dst.at[peer], send_sem=send_sem.at[peer],
            recv_sem=recv_sem.at[peer], device_id=(my_r, peer), device_id_type=MESH)
        copy.wait_send()
        copy.wait_recv()
        return carry

    lax.fori_loop(1, owners, wait, 0)


def exchange_kernel(regions, owners, face_ref, cots_ref, got_face_ref, got_cot_ref,
                    own, fsend, frecv, bsend, brecv, lsem):
    my_r = lax.axis_index("region")
    my_s = lax.axis_index("space")
    greet_region(regions, owners, my_r, my_s)
    send_faces(regions, owners, my_r, my_s, False, face_ref, got_face_ref, fsend, frecv)
    start_blocks(owners, my_r, my_s, cots_ref, got_cot_ref, bsend, brecv)
    take = pltpu.make_async_copy(cots_ref.at[my_s], own, lsem.at[0])
    take.start()
    take.wait()
    put = pltpu.make_async_copy(own, got_cot_ref.at[my_s], lsem.at[1])
    put.start()
    put.wait()
    wait_faces(regions, owners, my_r, my_s, False, face_ref, got_face_ref, fsend, frecv)
    wait_blocks(owners, my_r, my_s, cots_ref, got_cot_ref, bsend, brecv)


def silu_parts(v):
    s = 1.0 / (1.0 + jnp.exp(-v))
    return v * s, s * (1.0 + v * (1.0 - s))


def place(w_ref, base, q_in, q_out, block):
    w_ref[base + q_in * 64:base + q_in * 64 + 64, q_out * 64:q_out * 64 + 64] = block


def fill_weights(fine_ref, w_ref, wt_ref):
    w_ref[...] = jnp.zeros_like(w_ref)
    wt_ref[...] = jnp.zeros_like(wt_ref)
    same = [(q, q) for q in range(4)]
    up_j = [(0, 2), (1, 3)]
    down_j = [(2, 0), (3, 1)]
    up_k = [(0, 1), (2, 3)]
    down_k = [(1, 0), (3, 2)]
    plan = [
        (0, 0, 0, same), (1, 1, 2, same), (2, 2, 1, same),
        (3, 0, 0, up_j), (3, 3, 3, down_j), (4, 0, 0, down_j), (4, 3, 3, up_j),
        (5, 0, 0, up_k), (5, 4, 4, down_k), (6, 0, 0, down_k), (6, 4, 4, up_k),
    ]
    for tap, fwd, bwd, pairs in plan:
        w = fine_ref[tap]
        wt = w.astype(F32).T.astype(BF)
        for q_in, q_out in pairs:
            place(w_ref, fwd * 256, q_in, q_out, w)
            place(wt_ref, bwd * 256, q_out, q_in, wt)
    return plan


def compute_kernel(scale_fine, scale_coarse, code_ref, slot_ref, x_ref, table_ref, inf_ref,
                   cot_ref, fine_ref, down_ref, coarse_ref, shift_ref, back_ref,
                   gin_ref, fg_ref, bf_ref, co_ref, grad_ref,
                   w_ref, wt_ref, taps_ref, act_ref, gh_ref, red_ref, cg_ref, ch_ref):
    plan = fill_weights(fine_ref, w_ref, wt_ref)
    fg_ref[...] = jnp.zeros_like(fg_ref)
    bf_ref[...] = jnp.zeros_like(bf_ref)
    lane = lax.broadcasted_iota(jnp.int32, (ROWS, LANES), 1)
    k_low = (lane % 128) < 64
    k_low32 = k_low[0:32]
    face_total = table_ref.shape[0]

    def halo(b, d):
        code = code_ref[b, d]
        own = table_ref[jnp.clip(code, 0, face_total - 1)]
        got = inf_ref[jnp.clip(code - face_total, 0, inf_ref.shape[0] - 1)]
        picked = jnp.where(code >= face_total, got, own)
        return jnp.where(code >= 0, picked, jnp.zeros_like(picked))

    def one(b, carry):
        x = x_ref[b]
        h = [halo(b, d) for d in range(6)]
        hi_m = jnp.concatenate([h[0][0:16], h[0][16:32]], axis=1)
        hi_p = jnp.concatenate([h[1][0:16], h[1][16:32]], axis=1)
        hj = jnp.concatenate([h[3], h[2]], axis=1)
        hk = jnp.concatenate(
            [h[5][:, 0:64], h[4][:, 0:64], h[5][:, 64:128], h[4][:, 64:128]], axis=1)
        ext = jnp.concatenate([x, hj, hk], axis=0)
        tj = jnp.concatenate(
            [dot(shift_ref[0], ext[:, 0:128]), dot(shift_ref[1], ext[:, 128:256])], axis=1)
        tk = jnp.where(k_low, dot(shift_ref[2], ext), dot(shift_ref[3], ext))
        taps = jnp.concatenate([
            x,
            jnp.concatenate([hi_m, x[0:112]], axis=0),
            jnp.concatenate([x[16:128], hi_p], axis=0),
            tj.astype(BF), tk.astype(BF)], axis=1)
        row = pl.multiple_of(b * ROWS, ROWS)
        taps_ref[pl.ds(row, ROWS), :] = taps
        hidden = dot(taps, w_ref[...])
        act, slope = silu_parts(hidden)
        act = act.astype(BF)
        even = jnp.concatenate([act[32 * n:32 * n + 16] for n in range(4)], axis=0)
        odd = jnp.concatenate([act[32 * n + 16:32 * n + 32] for n in range(4)], axis=0)
        pair = jnp.concatenate([even, odd], axis=1)
        half = pl.multiple_of(b * 64, 64)
        act_ref[pl.ds(half, 64), :] = pair
        reduced = dot(pair, down_ref[...]).astype(BF)
        red_ref[pl.ds(half, 64), :] = reduced
        slot = slot_ref[b]
        c_out, c_slope = silu_parts(dot(reduced, coarse_ref[...]))
        co_ref[slot] = c_out.astype(BF)
        c_grad = (cot_ref[slot].astype(F32) * c_slope).astype(BF)
        cg_ref[pl.ds(half, 64), :] = c_grad
        child = dot(c_grad, coarse_ref[...], NT).astype(BF)
        ch_ref[pl.ds(half, 64), :] = child
        ga = dot(child, down_ref[...], NT)
        pieces = []
        for n in range(4):
            pieces += [ga[16 * n:16 * n + 16, 0:256], ga[16 * n:16 * n + 16, 256:512]]
        gh = (jnp.concatenate(pieces, axis=0) * slope).astype(BF)
        gh_ref[pl.ds(row, ROWS), :] = gh
        gj = jnp.concatenate(
            [dot(back_ref[0], gh[:, 0:128]), dot(back_ref[1], gh[:, 128:256])], axis=1).astype(BF)
        gk_low = dot(back_ref[2], gh)
        gk_high = dot(back_ref[3], gh)
        gk = jnp.where(k_low, gk_low[0:128], gk_high[0:128]).astype(BF)
        gkf = jnp.where(k_low32, gk_low[128:160], gk_high[128:160]).astype(BF)
        blank = jnp.zeros((16, LANES), BF)
        bwd = jnp.concatenate([
            gh,
            jnp.concatenate([blank, gh[0:112]], axis=0),
            jnp.concatenate([gh[16:128], blank], axis=0),
            gj[0:128], gk], axis=1)
        gin_ref[b] = dot(bwd, wt_ref[...])
        p0 = dot(gh[0:16], wt_ref[512:768, :]).astype(BF)
        p1 = dot(gh[112:128], wt_ref[256:512, :]).astype(BF)
        pj = dot(gj[128:160], wt_ref[768:1024, :]).astype(BF)
        pk = dot(gkf, wt_ref[1024:1280, :]).astype(BF)
        planes = [
            jnp.concatenate([p0[:, 0:128], p0[:, 128:256]], axis=0),
            jnp.concatenate([p1[:, 0:128], p1[:, 128:256]], axis=0),
            pj[:, 128:256],
            pj[:, 0:128],
            jnp.concatenate([pk[:, 64:128], pk[:, 192:256]], axis=1),
            jnp.concatenate([pk[:, 0:64], pk[:, 128:192]], axis=1),
        ]
        for d in range(6):
            code = code_ref[b, d]
            plane = planes[d]

            @pl.when(code >= face_total)
            def _():
                bf_ref[code - face_total] = plane

            @pl.when((code >= 0) & (code < face_total))
            def _():
                fg_ref[code] += plane.astype(F32)
        return carry

    lax.fori_loop(0, x_ref.shape[0], one, 0)
    fine = dot(taps_ref[...], gh_ref[...], TN) * scale_fine
    sums = [None] * 7
    for tap, fwd, bwd, pairs in plan:
        for q_in, q_out in pairs:
            part = fine[fwd * 256 + q_in * 64:fwd * 256 + q_in * 64 + 64,
                        q_out * 64:q_out * 64 + 64]
            sums[tap] = part if sums[tap] is None else sums[tap] + part
    sums.append(jnp.zeros_like(sums[0]))
    for n in range(4):
        grad_ref[n * 64:n * 64 + 64, :] = jnp.concatenate([sums[2 * n], sums[2 * n + 1]], axis=1)
    grad_ref[256:768, :] = dot(act_ref[...], ch_ref[...], TN) * scale_fine
    grad_ref[768:896, :] = dot(red_ref[...], cg_ref[...], TN) * scale_coarse


def greet_all(regions, owners, my_r, my_s):
    barrier = pltpu.get_barrier_semaphore()
    count = regions * owners
    me = my_r * owners + my_s

    def greet(step, carry):
        peer = lax.rem(me + step, count)
        pl.semaphore_signal(barrier, inc=1, device_id=(peer // owners, lax.rem(peer, owners)),
                            device_id_type=MESH)
        return carry

    lax.fori_loop(1, count, greet, 0)
    pl.semaphore_wait(barrier, count - 1)


def answer_kernel(regions, owners, face_ref, blocks_ref, grad_ref, got_face_ref, got_block_ref,
                  total_ref, own, parts, mine, fsend, frecv, bsend, brecv, lsem,
                  rsend, rrecv, gsend, grecv):
    my_r = lax.axis_index("region")
    my_s = lax.axis_index("space")
    count = regions * owners
    me = my_r * owners + my_s
    chunks = grad_ref.shape[0]
    greet_all(regions, owners, my_r, my_s)
    send_faces(regions, owners, my_r, my_s, True, face_ref, got_face_ref, fsend, frecv)

    def spot(peer):
        return (peer // owners, lax.rem(peer, owners))

    def reduce_copy(slot, peer):
        return pltpu.make_async_remote_copy(
            src_ref=grad_ref.at[jnp.minimum(peer, chunks - 1)], dst_ref=parts.at[slot],
            send_sem=rsend.at[peer], recv_sem=rrecv.at[slot], device_id=spot(peer),
            device_id_type=MESH)

    def gather_copy(chunk, peer):
        return pltpu.make_async_remote_copy(
            src_ref=mine, dst_ref=total_ref.at[jnp.minimum(chunk, chunks - 1)],
            send_sem=gsend.at[peer], recv_sem=grecv.at[chunk], device_id=spot(peer),
            device_id_type=MESH)

    def start_reduce(step, carry):
        peer = lax.rem(me + step, count)

        @pl.when(peer < chunks)
        def _():
            reduce_copy(me, peer).start()
        return carry

    lax.fori_loop(1, count, start_reduce, 0)
    start_blocks(owners, my_r, my_s, blocks_ref, got_block_ref, bsend, brecv)
    take = pltpu.make_async_copy(blocks_ref.at[my_s], own, lsem.at[0])
    take.start()

    def end_reduce(step, carry):
        peer = lax.rem(me + step, count)

        @pl.when(peer < chunks)
        def _():
            reduce_copy(me, peer).wait_send()

        @pl.when(me < chunks)
        def _():
            reduce_copy(peer, peer).wait_recv()
        return carry

    @pl.when(me < chunks)
    def _():
        keep = pltpu.make_async_copy(grad_ref.at[jnp.minimum(me, chunks - 1)], parts.at[me], lsem.at[2])
        keep.start()
        keep.wait()

    lax.fori_loop(1, count, end_reduce, 0)

    @pl.when(me < chunks)
    def _():
        mine[...] = lax.fori_loop(
            0, count, lambda n, acc: acc + parts[n], jnp.zeros_like(mine))

        def start_gather(step, carry):
            gather_copy(me, lax.rem(me + step, count)).start()
            return carry

        lax.fori_loop(1, count, start_gather, 0)
        total_ref[jnp.minimum(me, chunks - 1)] = mine[...]

    take.wait()
    put = pltpu.make_async_copy(own, got_block_ref.at[my_s], lsem.at[1])
    put.start()
    wait_faces(regions, owners, my_r, my_s, True, face_ref, got_face_ref, fsend, frecv)
    put.wait()

    def end_gather(step, carry):
        peer = lax.rem(me + step, count)

        @pl.when(me < chunks)
        def _():
            gather_copy(me, peer).wait_send()

        @pl.when(peer < chunks)
        def _():
            gather_copy(peer, peer).wait_recv()
        return carry

    lax.fori_loop(1, count, end_gather, 0)
    wait_blocks(owners, my_r, my_s, blocks_ref, got_block_ref, bsend, brecv)


def last_kernel(req_ref, slot_ref, gin_ref, fg_ref, ans_ref, arr_ref, order_ref, spread_ref,
                grad_ref, out_ref, fg_acc):
    fg_acc[...] = fg_ref[...]
    for s in range(24):
        want = req_ref[0, s]

        @pl.when(want >= 0)
        def _():
            fg_acc[want] += ans_ref[s].astype(F32)

    out_ref[...] = jnp.zeros_like(out_ref)

    def put_block(s, carry):
        spot = slot_ref[0, s]

        @pl.when(spot >= 0)
        def _():
            out_ref[spot] = arr_ref[s]
        return carry

    lax.fori_loop(0, 64, put_block, 0)
    lane = lax.broadcasted_iota(jnp.int32, (32, LANES), 1)
    k_low = (lane % 128) < 64

    def split(v):
        high = v.astype(BF)
        return high, (v - high.astype(F32)).astype(BF)

    def one(b, carry):
        base = b * 6
        f = [fg_acc[base + n] for n in range(6)]
        j_sum = jnp.concatenate([f[2], f[3]], axis=1)
        k_sum = jnp.concatenate(
            [f[4][:, 0:64], f[5][:, 0:64], f[4][:, 64:128], f[5][:, 64:128]], axis=1)
        zero = jnp.zeros_like(k_sum)
        parts = split(j_sum) + split(jnp.where(k_low, k_sum, zero)) + split(
            jnp.where(k_low, zero, k_sum))
        stack = jnp.concatenate(parts, axis=0)
        spread = jnp.concatenate(
            [dot(spread_ref[0], stack[:, 0:128]), dot(spread_ref[1], stack[:, 128:256])], axis=1)
        total = gin_ref[b] + spread
        low = jnp.concatenate([f[0][0:16], f[0][16:32]], axis=1)
        high = jnp.concatenate([f[1][0:16], f[1][16:32]], axis=1)
        total = jnp.concatenate(
            [total[0:16] + low, total[16:112], total[112:128] + high], axis=0)
        turned = total.T.astype(BF)
        wide = jnp.concatenate([turned[q * 64:q * 64 + 64] for q in range(4)], axis=1)
        grad_ref[b] = dot(wide, order_ref[...]).astype(BF)
        return carry

    lax.fori_loop(0, gin_ref.shape[0], one, 0)


def on_device(features, fine_weight, down_weight, coarse_weight, cotangent, face_source,
              face_requests, child_slot, parent_octant):
    regions = lax.axis_size("region")
    owners = lax.axis_size("space")
    count = regions * owners
    bricks, channels, volume = features.shape
    faces = bricks * 6
    parents, _, wide = cotangent.shape
    octant = volume // 8
    slots = parent_octant.shape[1]
    shape = jax.ShapeDtypeStruct
    big = pltpu.CompilerParams(vmem_limit_bytes=60 * 2**20)
    x, table, out_faces, out_cots = pl.pallas_call(
        first_kernel,
        out_shape=(shape((bricks, ROWS, LANES), BF), shape((faces, 32, 128), BF),
                   shape((24, 32, 128), BF), shape((slots, octant, wide), BF)),
        in_specs=[SMEM_SPEC] * 2 + [VMEM_SPEC] * 4,
        out_specs=(VMEM_SPEC,) * 4,
        compiler_params=big,
        name="first",
    )(face_requests, parent_octant, features, cotangent.reshape(parents * 8, octant, wide),
      jnp.asarray(ORDER), jnp.asarray(FACE))
    pair = slots // owners
    dma = pltpu.SemaphoreType.DMA
    in_faces, in_cots = pl.pallas_call(
        functools.partial(exchange_kernel, regions, owners),
        out_shape=(shape((6, 4, 32, 128), BF), shape((owners, pair, octant, wide), BF)),
        in_specs=[ANY_SPEC] * 2,
        out_specs=(ANY_SPEC,) * 2,
        scratch_shapes=[pltpu.VMEM((pair, octant, wide), BF), dma((6,)), dma((6,)),
                        dma((owners,)), dma((owners,)), dma((2,))],
        compiler_params=pltpu.CompilerParams(collective_id=0, has_side_effects=True),
        name="exchange",
    )(out_faces.reshape(6, 4, 32, 128), out_cots.reshape(owners, pair, octant, wide))
    scale_fine = 1.0 / math.sqrt(bricks * count * volume)
    scale_coarse = 1.0 / math.sqrt(parents * count * volume)
    gin, fg, back, co, grads = pl.pallas_call(
        functools.partial(compute_kernel, scale_fine, scale_coarse),
        out_shape=(shape((bricks, ROWS, LANES), F32), shape((faces, 32, 128), F32),
                   shape((24, 32, 128), BF), shape((slots, octant, wide), BF),
                   shape((896, 128), F32)),
        in_specs=[SMEM_SPEC] * 2 + [VMEM_SPEC] * 9,
        out_specs=(VMEM_SPEC,) * 5,
        scratch_shapes=[
            pltpu.VMEM((1280, LANES), BF), pltpu.VMEM((1280, LANES), BF),
            pltpu.VMEM((bricks * ROWS, 1280), BF), pltpu.VMEM((bricks * 64, 512), BF),
            pltpu.VMEM((bricks * ROWS, LANES), BF), pltpu.VMEM((bricks * 64, wide), BF),
            pltpu.VMEM((bricks * 64, wide), BF), pltpu.VMEM((bricks * 64, wide), BF)],
        compiler_params=big,
        name="compute",
    )(face_source, child_slot, x, table, in_faces.reshape(24, 32, 128),
      in_cots.reshape(slots, octant, wide), fine_weight,
      down_weight.reshape(8 * channels, wide), coarse_weight,
      jnp.asarray(SHIFT), jnp.asarray(BACK))
    chunk = max(CHUNK, 896 // count)
    chunks = 896 // chunk
    answers, arrived, totals = pl.pallas_call(
        functools.partial(answer_kernel, regions, owners),
        out_shape=(shape((6, 4, 32, 128), BF), shape((owners, pair, octant, wide), BF),
                   shape((chunks, chunk, 128), F32)),
        in_specs=[ANY_SPEC, ANY_SPEC, VMEM_SPEC],
        out_specs=(ANY_SPEC, ANY_SPEC, VMEM_SPEC),
        scratch_shapes=[pltpu.VMEM((pair, octant, wide), BF),
                        pltpu.VMEM((count, chunk, 128), F32), pltpu.VMEM((chunk, 128), F32),
                        dma((6,)), dma((6,)), dma((owners,)), dma((owners,)), dma((3,)),
                        dma((count,)), dma((count,)), dma((count,)), dma((count,))],
        compiler_params=pltpu.CompilerParams(collective_id=1, has_side_effects=True),
        name="answer",
    )(back.reshape(6, 4, 32, 128), co.reshape(owners, pair, octant, wide),
      grads.reshape(chunks, chunk, 128))
    grad_in, coarse_out = pl.pallas_call(
        last_kernel,
        out_shape=(shape((bricks, channels, volume), BF), shape((parents * 8, octant, wide), BF)),
        in_specs=[SMEM_SPEC] * 2 + [VMEM_SPEC] * 6,
        out_specs=(VMEM_SPEC,) * 2,
        scratch_shapes=[pltpu.VMEM((faces, 32, 128), F32)],
        compiler_params=big,
        name="last",
    )(face_requests, parent_octant, gin, fg, answers.reshape(24, 32, 128),
      arrived.reshape(slots, octant, wide), jnp.asarray(ORDER), jnp.asarray(SPREAD))
    totals = totals.reshape(896, 128)
    fine = totals[0:256].reshape(4, 64, 2, 64).transpose(0, 2, 1, 3).reshape(8, 64, 64)[0:7]
    return (grad_in, coarse_out.reshape(parents, volume, wide), fine,
            totals[256:768].reshape(8, channels, wide), totals[768:896])


def solution(mesh):
    both = ("region", "space")
    return jax.shard_map(
        on_device,
        mesh=mesh,
        in_specs=(P(both, None, None), P(), P(), P(), P(both, None, None), P(both, None),
                  P(both, None), P(both), P(both, None)),
        out_specs=(P(both, None, None), P(both, None, None), P(), P(), P()),
        check_vma=False,
    )
```

profile of v0, /device:TPU:1, one launch (start us, length us, event | category | flops | bytes accessed | tf_op | source)
XLA Modules:
  0.0 121.9 jit_solution(6566545466610543753)
XLA Ops:
  0.6 1.4 %copy.19.code_ref = s32[16,6]{1,0:T(8,128)} copy(s32[16,6]{0,1:T(8,128)} %param.19) | data formatting | bytes 768 | tf_op args[5]
  2.0 6.7 %first.1 = (bf16[16,128,256]{2,1,0:T(8,128)(2,1)}, bf16[96,32,128]{2,1,0:T(8,128)(2,1)}, bf16[24,32,128]{2,1,0:T(8,128)(2,1)}, bf16[64,64,128]{2,1,0:T(8,128)(2,1)}) custom-call(s32[1,24]{1,0:T(1,128)} %req_ref.3, s32[1,64]{1,0:T(1,128)} %slot_ref.5, bf16[16,64,512]{2,1,0:T(8,128)(2,1)} %feat_ref.1, bf16[64,64,128]{2,1,0:T(8,128)(2,1)} %bitcast.17, ...), custom_call_target="tpu_custom_call" | custom-call | tf_op jit(solution)/shard_map/first/pallas_call | solution.py:532
  8.7 25.1 %exchange.1 = (bf16[6,4,32,128]{3,2,1,0:T(8,128)(2,1)}, bf16[32,2,64,128]{3,2,1,0:T(8,128)(2,1)}) custom-call(bf16[6,4,32,128]{3,2,1,0:T(8,128)(2,1)} %bitcast.28, bf16[32,2,64,128]{3,2,1,0:T(8,128)(2,1)} %bitcast.18), custom_call_target="tpu_custom_call" | custom-call | tf_op jit(solution)/shard_map/exchange/pallas_call | solution.py:544
  33.9 29.0 %compute.1 = (f32[16,128,256]{2,1,0:T(8,128)}, f32[96,32,128]{2,1,0:T(8,128)}, bf16[24,32,128]{2,1,0:T(8,128)(2,1)}, bf16[64,64,128]{2,1,0:T(8,128)(2,1)}, f32[896,128]{1,0:T(8,128)}) custom-call(s32[16,6]{1,0:T(8,128)} %copy.19.code_ref, s32[16]{0:T(128)} %slot_ref.4, bf16[16,128,256]{2,1,0:T(8,128)(2,1)} %get-tuple-element.21.x_ref, ...), custom_call_target="tpu_custom_call" | custom-call | tf_op jit(solution)/shard_map/compute/pallas_call | solution.py:556
  62.9 44.2 %answer.1 = (bf16[6,4,32,128]{3,2,1,0:T(8,128)(2,1)}, bf16[32,2,64,128]{3,2,1,0:T(8,128)(2,1)}, f32[112,8,128]{2,1,0:T(8,128)}) custom-call(bf16[6,4,32,128]{3,2,1,0:T(8,128)(2,1)} %bitcast.29, bf16[32,2,64,128]{3,2,1,0:T(8,128)(2,1)} %bitcast.20, f32[112,8,128]{2,1,0:T(8,128)} %bitcast.24), custom_call_target="tpu_custom_call" | custom-call | tf_op jit(solution)/shard_map/answer/pallas_call | solution.py:576
  107.1 0.0 copy-start
  107.1 12.6 %last.1 = (bf16[16,64,512]{2,1,0:T(8,128)(2,1)}, bf16[64,64,128]{2,1,0:T(8,128)(2,1)}) custom-call(s32[1,24]{1,0:T(1,128)} %req_ref.3, s32[1,64]{1,0:T(1,128)} %slot_ref.5, f32[16,128,256]{2,1,0:T(8,128)} %get-tuple-element.27.gin_ref, f32[96,32,128]{2,1,0:T(8,128)} %get-tuple-element.28.fg_ref, bf16[24,32,128]{2,1,0:T(8,128)(2,1)} %bitcast.27, ...), custom_call_target="tpu_custom_call" | custom-call | tf_op jit(solution)/shard_map/last/pallas_call | solution.py:590
  119.6 0.0 copy-done
  119.7 0.6 slice_bitcast_fusion
  120.3 0.7 slice.19
  121.0 0.2 reshape.73
  121.2 0.7 slice.22
  (2 shorter events, 0.0 us)
Async XLA Ops:
  107.1 12.6 %copy-start = (f32[112,8,128]{2,1,0:T(8,128)S(1)}, f32[112,8,128]{2,1,0:T(8,128)}, u32[]{:S(2)}) copy-start(f32[112,8,128]{2,1,0:T(8,128)} %get-tuple-element.36) | copy-start | bytes 1376260
where the time goes:
time: 123 us; the launch traced here: 122 us
  Pallas kernels  118 us (96%)
  local copies, waits for them, and re-layouts  3.64 us (3%)
    pallas_call x1, Pallas kernels, on_device(): pl.pallas_call(functools.partial(answer_kernel, regions, owners), out_sha...  44.2 us
    pallas_call x1, Pallas kernels, on_device(): pl.pallas_call(functools.partial(compute_kernel, scale_fine, scale_coarse...  29 us
    pallas_call x1, Pallas kernels, on_device(): pl.pallas_call(functools.partial(exchange_kernel, regions, owners), out_s...  25.1 us
    pallas_call x1, Pallas kernels, on_device(): pl.pallas_call(last_kernel, out_shape=(shape((bricks, channels, volume),...  12.6 us
    pallas_call x1, Pallas kernels, on_device(): pl.pallas_call(first_kernel, out_shape=(shape((bricks, ROWS, LANES), BF),...  6.73 us

commit v1 on v0

v1 whole, which is shorter than its diff:
```python
import functools
import math

import jax
import jax.numpy as jnp
import numpy as np
from jax import lax
from jax.experimental import pallas as pl
from jax.experimental.pallas import tpu as pltpu
from jax.sharding import PartitionSpec as P

EDGE = 8
BF = jnp.bfloat16
F32 = jnp.float32
MESH = pl.DeviceIdType.MESH
NT = (((1,), (1,)), ((), ()))
TN = (((0,), (0,)), ((), ()))
VMEM_SPEC = pl.BlockSpec(memory_space=pltpu.VMEM)
SMEM_SPEC = pl.BlockSpec(memory_space=pltpu.SMEM)
ANY_SPEC = pl.BlockSpec(memory_space=pl.ANY)
ROWS = 128
LANES = 256
GROUP = 4


def row_of(i, j, k):
    return i * 16 + j * 4 + k


def make_tables():
    order = np.zeros((512, 512), np.float32)
    for i in range(8):
        for j in range(8):
            for k in range(8):
                q = (j % 2) * 2 + k % 2
                order[q * 128 + row_of(i, j // 2, k // 2), i * 64 + j * 8 + k] = 1
    face = np.zeros((128, 128), np.float32)
    for i in range(8):
        for m in range(4):
            face[i * 4 + m, row_of(i, 0, m)] = 1
            face[32 + i * 4 + m, row_of(i, 3, m)] = 1
            face[64 + i * 4 + m, row_of(i, m, 0)] = 1
            face[96 + i * 4 + m, row_of(i, m, 3)] = 1
    spread = np.zeros((2, 128, 192), np.float32)
    for half in range(2):
        j_face = face[0:32] if half == 0 else face[32:64]
        parts = [j_face, j_face, face[64:96], face[64:96], face[96:128], face[96:128]]
        spread[half] = np.concatenate(parts, axis=0).T
    cast = lambda a: np.asarray(a, dtype=BF)
    return cast(order), cast(face), cast(spread)


ORDER, FACE, SPREAD = make_tables()


def dot(a, b, dims=(((1,), (0,)), ((), ()))):
    return lax.dot_general(a, b, dims, preferred_element_type=F32)


def neighbours(regions, owners):
    far = owners // 4
    return [(1, 0), (-1, 0), (0, 1), (0, -1), (0, far), (0, -far)]


def face_moves(regions, owners, my_r, my_s, backward):
    sign = -1 if backward else 1
    for k, (dr, ds) in enumerate(neighbours(regions, owners)):
        to_r, to_s = my_r + sign * dr, my_s + sign * ds
        from_r, from_s = my_r - sign * dr, my_s - sign * ds
        can_send = (to_r >= 0) & (to_r < regions) & (to_s >= 0) & (to_s < owners)
        can_take = (from_r >= 0) & (from_r < regions) & (from_s >= 0) & (from_s < owners)
        yield k, (to_r, to_s), can_send, can_take


def send_faces(regions, owners, my_r, my_s, backward, src, dst, send_sem, recv_sem):
    for k, target, can_send, can_take in face_moves(regions, owners, my_r, my_s, backward):
        copy = pltpu.make_async_remote_copy(
            src_ref=src.at[k], dst_ref=dst.at[k], send_sem=send_sem.at[k],
            recv_sem=recv_sem.at[k], device_id=target, device_id_type=MESH)

        @pl.when(can_send)
        def _():
            copy.start()


def wait_faces(regions, owners, my_r, my_s, backward, src, dst, send_sem, recv_sem):
    for k, target, can_send, can_take in face_moves(regions, owners, my_r, my_s, backward):
        copy = pltpu.make_async_remote_copy(
            src_ref=src.at[k], dst_ref=dst.at[k], send_sem=send_sem.at[k],
            recv_sem=recv_sem.at[k], device_id=target, device_id_type=MESH)

        @pl.when(can_send)
        def _():
            copy.wait_send()

        @pl.when(can_take)
        def _():
            copy.wait_recv()


def block_copy(my_r, peer, pair, take, land, src, dst, send_sem, recv_sem):
    return pltpu.make_async_remote_copy(
        src_ref=src.at[pl.ds(take * pair, pair)], dst_ref=dst.at[pl.ds(land * pair, pair)],
        send_sem=send_sem.at[take], recv_sem=recv_sem.at[land], device_id=(my_r, peer),
        device_id_type=MESH)


def start_blocks(owners, my_r, my_s, pair, src, dst, send_sem, recv_sem):
    def start(step, carry):
        peer = lax.rem(my_s + step, owners)
        block_copy(my_r, peer, pair, peer, my_s, src, dst, send_sem, recv_sem).start()
        return carry

    lax.fori_loop(1, owners, start, 0)


def wait_blocks(owners, my_r, my_s, pair, src, dst, send_sem, recv_sem):
    def wait(step, carry):
        peer = lax.rem(my_s + step, owners)
        copy = block_copy(my_r, peer, pair, peer, peer, src, dst, send_sem, recv_sem)
        copy.wait_send()
        copy.wait_recv()
        return carry

    lax.fori_loop(1, owners, wait, 0)


def silu_parts(v):
    s = 1.0 / (1.0 + jnp.exp(-v))
    return v * s, s * (1.0 + v * (1.0 - s))


def place(w_ref, base, q_in, q_out, block):
    w_ref[base + q_in * 64:base + q_in * 64 + 64, q_out * 64:q_out * 64 + 64] = block


def fill_weights(fine_ref, w_ref, wt_ref):
    w_ref[...] = jnp.zeros_like(w_ref)
    wt_ref[...] = jnp.zeros_like(wt_ref)
    same = [(q, q) for q in range(4)]
    up_j = [(0, 2), (1, 3)]
    down_j = [(2, 0), (3, 1)]
    up_k = [(0, 1), (2, 3)]
    down_k = [(1, 0), (3, 2)]
    plan = [
        (0, 0, 0, same), (1, 1, 2, same), (2, 2, 1, same),
        (3, 0, 0, up_j), (3, 3, 3, down_j), (4, 0, 0, down_j), (4, 3, 3, up_j),
        (5, 0, 0, up_k), (5, 4, 4, down_k), (6, 0, 0, down_k), (6, 4, 4, up_k),
    ]
    for tap, fwd, bwd, pairs in plan:
        w = fine_ref[tap]
        wt = w.astype(F32).T.astype(BF)
        for q_in, q_out in pairs:
            place(w_ref, fwd * 256, q_in, q_out, w)
            place(wt_ref, bwd * 256, q_out, q_in, wt)
    return plan


def index_kernel(code_ref, slot_ref, child_ref, face_ref):
    for s in range(child_ref.shape[0]):
        child_ref[s] = 0
    for s in range(face_ref.shape[0]):
        face_ref[s] = 0
    for b in range(slot_ref.shape[0]):
        child_ref[slot_ref[b]] = b
    total = code_ref.shape[0]

    def mark(n, carry):
        code = code_ref[n]

        @pl.when(code >= total)
        def _():
            face_ref[code - total] = n
        return carry

    lax.fori_loop(0, total, mark, 0, unroll=8)


def signal_peers(regions, owners, my_r, my_s):
    barrier = pltpu.get_barrier_semaphore()
    core = lax.rem(my_s, 2)
    half = owners // 2

    def greet(step, carry):
        peer = lax.rem(my_s + step, owners)
        pl.semaphore_signal(barrier, inc=1, device_id=(my_r, peer), device_id_type=MESH)
        return carry

    lax.fori_loop(1, owners, greet, 0)

    def greet_far(step, carry):
        far_r = lax.rem(my_r + 1 + step // half, regions)
        far_s = 2 * lax.rem(step, half) + core
        pl.semaphore_signal(barrier, inc=1, device_id=(far_r, far_s), device_id_type=MESH)
        return carry

    lax.fori_loop(0, (regions - 1) * half, greet_far, 0)


def wait_peers(regions, owners):
    barrier = pltpu.get_barrier_semaphore()
    pl.semaphore_wait(barrier, owners - 1 + (regions - 1) * (owners // 2))


def row_roll(v, by):
    return pltpu.roll(v, by % v.shape[0], 0)


def pieces8(v, start, step, count):
    return jnp.concatenate([v[start + n * step:start + n * step + 8] for n in range(count)], axis=0)


def main_kernel(regions, owners, scale_fine, scale_coarse,
                code_ref, slot_ref, req_ref, po_ref, child_inv, face_inv,
                feat_hbm, cot_hbm, order_hbm, face_ref, fine_ref, down_ref, coarse_ref,
                gin_ref, plane_ref, ans_ref, blocks_out, total_ref,
                feat, cot, order, x_ref, table, out_face, in_face, cots, got_cots,
                w_ref, wt_ref, taps_ref, act_ref, gh_ref, red_ref, cg_ref, ch_ref,
                co_ref, co_slots, slope_ref, cslope_ref, back_face, halo_scr, g_scr,
                grads, pair_got, half_sum, parts, mine,
                load, fsend, frecv, bsend, brecv, hsend, hrecv, csend, crecv, osem,
                psend, precv, rsend, rrecv, gsend, grecv):
    my_r = lax.axis_index("region")
    my_s = lax.axis_index("space")
    bricks = feat.shape[0]
    face_total = table.shape[0]
    slots = cots.shape[0]
    pair = slots // owners
    loads = [pltpu.make_async_copy(src, dst, load.at[n]) for n, (src, dst) in enumerate(
        [(feat_hbm, feat), (order_hbm, order), (cot_hbm, cot)])]
    for copy in loads:
        copy.start()
    signal_peers(regions, owners, my_r, my_s)
    plan = fill_weights(fine_ref, w_ref, wt_ref)
    loads[0].wait()
    loads[1].wait()

    def turn(g, carry):
        block = feat[pl.ds(g * GROUP, GROUP)].reshape(GROUP * 64, 512)
        turned = dot(order[...], block, NT).astype(BF)
        for n in range(GROUP):
            b = g * GROUP + n
            x = jnp.concatenate(
                [turned[q * 128:(q + 1) * 128, n * 64:(n + 1) * 64] for q in range(4)], axis=1
            )
            x_ref[pl.ds(b * ROWS, ROWS), :] = x
            f = dot(face_ref[...], x).astype(BF)
            base = b * 6
            table[base] = jnp.concatenate([x[0:16, 0:128], x[0:16, 128:256]], axis=0)
            table[base + 1] = jnp.concatenate([x[112:128, 0:128], x[112:128, 128:256]], axis=0)
            table[base + 2] = f[0:32, 0:128]
            table[base + 3] = f[32:64, 128:256]
            table[base + 4] = jnp.concatenate([f[64:96, 0:64], f[64:96, 128:192]], axis=1)
            table[base + 5] = jnp.concatenate([f[96:128, 64:128], f[96:128, 192:256]], axis=1)
        return carry

    lax.fori_loop(0, bricks // GROUP, turn, 0)
    for s in range(24):
        out_face[s // 4, s % 4] = table[jnp.maximum(req_ref[s], 0)]
    loads[2].wait()

    def gather_cot(s, carry):
        cots[s] = cot[jnp.maximum(po_ref[s], 0)]
        return carry

    lax.fori_loop(0, slots, gather_cot, 0, unroll=8)
    wait_peers(regions, owners)
    send_faces(regions, owners, my_r, my_s, False, out_face, in_face, fsend, frecv)
    start_blocks(owners, my_r, my_s, pair, cots, got_cots, bsend, brecv)
    for u in range(pair):
        got_cots[my_s * pair + u] = cots[my_s * pair + u]
    wait_faces(regions, owners, my_r, my_s, False, out_face, in_face, fsend, frecv)

    row8 = lax.broadcasted_iota(jnp.int32, (ROWS, 128), 0)
    first_j = lax.rem(row8, 16) < 4
    last_j = lax.rem(row8, 16) >= 12
    row_w = lax.broadcasted_iota(jnp.int32, (ROWS, LANES), 0)
    lane_w = lax.broadcasted_iota(jnp.int32, (ROWS, LANES), 1)
    k_low = lax.rem(lane_w, 128) < 64
    edge_k = lax.rem(row_w, 4) == jnp.where(k_low, 3, 0)
    low4 = lax.rem(lax.broadcasted_iota(jnp.int32, (32, 128), 0), 8) < 4

    def halo(b, d):
        code = code_ref[b * 6 + d]
        own = table[jnp.clip(code, 0, face_total - 1)]
        slot = jnp.clip(code - face_total, 0, 23)
        got = in_face[slot // 4, lax.rem(slot, 4)]
        picked = jnp.where(code >= face_total, got, own)
        return jnp.where(code >= 0, picked, jnp.zeros_like(picked))

    def shift_j(low, high):
        return row_roll(low, -4), row_roll(high, 4)

    def shift_k(v):
        return jnp.where(k_low, row_roll(v, -1), row_roll(v, 1))

    def forward_taps(b):
        row = pl.multiple_of(b * ROWS, ROWS)
        x = x_ref[pl.ds(row, ROWS), :]
        h = [halo(b, d) for d in range(6)]
        x32 = x.astype(F32)
        up, down = h[3].astype(F32), h[2].astype(F32)
        up_r, down_r = row_roll(up, 4), row_roll(down, -4)
        h_up, h_down = [], []
        for i in range(8):
            n = (i // 2) * 8
            a = (up_r if i % 2 == 0 else up)[n:n + 8]
            c = (down if i % 2 == 0 else down_r)[n:n + 8]
            h_up += [a, a]
            h_down += [c, c]
        low, high = shift_j(x32[:, 0:128], x32[:, 128:256])
        tj = jnp.concatenate([
            jnp.where(last_j, jnp.concatenate(h_up, axis=0), low),
            jnp.where(first_j, jnp.concatenate(h_down, axis=0), high)], axis=1)
        k5, k4 = h[5].astype(F32), h[4].astype(F32)
        k5r, k4r = pltpu.roll(k5, 64, 1), pltpu.roll(k4, 64, 1)
        halo_scr[0, pl.ds(3, 32, stride=4), :] = k5
        halo_scr[1, pl.ds(3, 32, stride=4), :] = k5r
        halo_scr[0, pl.ds(0, 32, stride=4), :] = k4r
        halo_scr[1, pl.ds(0, 32, stride=4), :] = k4
        hk = jnp.concatenate([halo_scr[0], halo_scr[1]], axis=1)
        tk = jnp.where(edge_k, hk, shift_k(x32))
        hi_m = jnp.concatenate([h[0][0:16], h[0][16:32]], axis=1)
        hi_p = jnp.concatenate([h[1][0:16], h[1][16:32]], axis=1)
        taps_ref[pl.ds(row, ROWS), :] = jnp.concatenate([
            x,
            jnp.concatenate([hi_m, x[0:112]], axis=0),
            jnp.concatenate([x[16:128], hi_p], axis=0),
            tj.astype(BF), tk.astype(BF)], axis=1)

    def forward(g, carry):
        for n in range(GROUP):
            forward_taps(g * GROUP + n)
        row = pl.multiple_of(g * GROUP * ROWS, GROUP * ROWS)
        half = pl.multiple_of(g * GROUP * 64, GROUP * 64)
        hidden = dot(taps_ref[pl.ds(row, GROUP * ROWS), :], w_ref[...])
        act, slope = silu_parts(hidden)
        slope_ref[pl.ds(row, GROUP * ROWS), :] = slope
        act = act.astype(BF)
        count = GROUP * 4
        even = jnp.concatenate([act[32 * n:32 * n + 16] for n in range(count)], axis=0)
        odd = jnp.concatenate([act[32 * n + 16:32 * n + 32] for n in range(count)], axis=0)
        both = jnp.concatenate([even, odd], axis=1)
        act_ref[pl.ds(half, GROUP * 64), :] = both
        reduced = dot(both, down_ref[...]).astype(BF)
        red_ref[pl.ds(half, GROUP * 64), :] = reduced
        c_out, c_slope = silu_parts(dot(reduced, coarse_ref[...]))
        co_ref[pl.ds(g * GROUP, GROUP)] = c_out.astype(BF).reshape(GROUP, 64, 128)
        cslope_ref[pl.ds(half, GROUP * 64), :] = c_slope
        return carry

    lax.fori_loop(0, bricks // GROUP, forward, 0)

    def gather_out(s, carry):
        co_slots[s] = co_ref[child_inv[s]]
        return carry

    lax.fori_loop(0, slots, gather_out, 0, unroll=8)
    wait_blocks(owners, my_r, my_s, pair, cots, got_cots, bsend, brecv)
    start_blocks(owners, my_r, my_s, pair, co_slots, blocks_out, csend, crecv)
    keep = pltpu.make_async_copy(co_slots.at[pl.ds(my_s * pair, pair)],
                                 blocks_out.at[pl.ds(my_s * pair, pair)], osem)
    keep.start()

    def backward(g, carry):
        row = pl.multiple_of(g * GROUP * ROWS, GROUP * ROWS)
        half = pl.multiple_of(g * GROUP * 64, GROUP * 64)
        cot_rows = jnp.concatenate(
            [got_cots[slot_ref[g * GROUP + n]] for n in range(GROUP)], axis=0).astype(F32)
        c_grad = (cot_rows * cslope_ref[pl.ds(half, GROUP * 64), :]).astype(BF)
        cg_ref[pl.ds(half, GROUP * 64), :] = c_grad
        child = dot(c_grad, coarse_ref[...], NT).astype(BF)
        ch_ref[pl.ds(half, GROUP * 64), :] = child
        ga = dot(child, down_ref[...], NT)
        rows = []
        for n in range(GROUP * 4):
            rows += [ga[16 * n:16 * n + 16, 0:256], ga[16 * n:16 * n + 16, 256:512]]
        all_gh = (jnp.concatenate(rows, axis=0) * slope_ref[pl.ds(row, GROUP * ROWS), :]).astype(BF)
        gh_ref[pl.ds(row, GROUP * ROWS), :] = all_gh
        bwd, f0, f1, fj, fk = [], [], [], [], []
        for n in range(GROUP):
            gh = all_gh[n * ROWS:(n + 1) * ROWS]
            g32 = gh.astype(F32)
            low, high = shift_j(g32[:, 0:128], g32[:, 128:256])
            zero = jnp.zeros_like(low)
            gj = jnp.concatenate(
                [jnp.where(last_j, zero, low), jnp.where(first_j, zero, high)], axis=1)
            gk = jnp.where(edge_k, jnp.zeros_like(g32), shift_k(g32))
            blank = jnp.zeros((16, LANES), BF)
            bwd.append(jnp.concatenate([
                gh,
                jnp.concatenate([blank, gh[0:112]], axis=0),
                jnp.concatenate([gh[16:128], blank], axis=0),
                gj.astype(BF), gk.astype(BF)], axis=1))
            f0.append(gh[0:16])
            f1.append(gh[112:128])
            j0 = jnp.where(low4, pieces8(g32[:, 0:128], 0, 32, 4),
                           row_roll(pieces8(g32[:, 0:128], 16, 32, 4), 4))
            j3 = jnp.where(low4, row_roll(pieces8(g32[:, 128:256], 8, 32, 4), -4),
                           pieces8(g32[:, 128:256], 24, 32, 4))
            fj.append(jnp.concatenate([j0, j3], axis=1).astype(BF))
            g_scr[0] = g32[:, 0:128]
            g_scr[1] = g32[:, 128:256]
            sides = []
            for side in range(2):
                sides.append(jnp.where(
                    k_low[0:32, 0:128], g_scr[side, pl.ds(0, 32, stride=4), :],
                    g_scr[side, pl.ds(3, 32, stride=4), :]))
            fk.append(jnp.concatenate(sides, axis=1).astype(BF))
        gin_ref[pl.ds(row, GROUP * ROWS), :] = dot(jnp.concatenate(bwd, axis=0), wt_ref[...])
        p0 = dot(jnp.concatenate(f0, axis=0), wt_ref[512:768, :]).astype(BF)
        p1 = dot(jnp.concatenate(f1, axis=0), wt_ref[256:512, :]).astype(BF)
        pj = dot(jnp.concatenate(fj, axis=0), wt_ref[768:1024, :]).astype(BF)
        pk = dot(jnp.concatenate(fk, axis=0), wt_ref[1024:1280, :]).astype(BF)
        for n in range(GROUP):
            base = (g * GROUP + n) * 6
            a, c = p0[n * 16:n * 16 + 16], p1[n * 16:n * 16 + 16]
            j, k = pj[n * 32:n * 32 + 32], pk[n * 32:n * 32 + 32]
            plane_ref[base] = jnp.concatenate([a[:, 0:128], a[:, 128:256]], axis=0)
            plane_ref[base + 1] = jnp.concatenate([c[:, 0:128], c[:, 128:256]], axis=0)
            plane_ref[base + 2] = j[:, 128:256]
            plane_ref[base + 3] = j[:, 0:128]
            plane_ref[base + 4] = jnp.concatenate([k[:, 64:128], k[:, 192:256]], axis=1)
            plane_ref[base + 5] = jnp.concatenate([k[:, 0:64], k[:, 128:192]], axis=1)
        return carry

    lax.fori_loop(0, bricks // GROUP, backward, 0)
    for s in range(24):
        back_face[s // 4, s % 4] = plane_ref[face_inv[s]]
    fine = dot(taps_ref[...], gh_ref[...], TN) * scale_fine
    send_faces(regions, owners, my_r, my_s, True, back_face, ans_ref, hsend, hrecv)
    sums = [None] * 7
    for tap, fwd, bwd, pairs in plan:
        for q_in, q_out in pairs:
            part = fine[fwd * 256 + q_in * 64:fwd * 256 + q_in * 64 + 64,
                        q_out * 64:q_out * 64 + 64]
            sums[tap] = part if sums[tap] is None else sums[tap] + part
    sums.append(jnp.zeros_like(sums[0]))

    def put_rows(start, value):
        count = value.shape[0] // 8
        grads[start // 8:start // 8 + count] = value.reshape(count, 8, 128)

    for n in range(4):
        put_rows(n * 64, jnp.concatenate([sums[2 * n], sums[2 * n + 1]], axis=1))
    put_rows(256, dot(act_ref[...], ch_ref[...], TN) * scale_fine)
    put_rows(768, dot(red_ref[...], cg_ref[...], TN) * scale_coarse)
    reduce_all(regions, owners, my_r, my_s, grads, pair_got, half_sum, parts, mine, total_ref,
               psend, precv, rsend, rrecv, gsend, grecv)
    wait_faces(regions, owners, my_r, my_s, True, back_face, ans_ref, hsend, hrecv)
    keep.wait()
    wait_blocks(owners, my_r, my_s, pair, co_slots, blocks_out, csend, crecv)


def reduce_all(regions, owners, my_r, my_s, grads, pair_got, half_sum, parts, mine, total_ref,
               psend, precv, rsend, rrecv, gsend, grecv):
    core = lax.rem(my_s, 2)
    other = 1 - core
    half = pair_got.shape[0]
    chips = parts.shape[0]
    width = owners // 2
    chip = my_r * width + my_s // 2
    rows = half_sum.shape[1]
    used = half_sum.shape[0]
    partner = (my_r, my_s + 1 - 2 * core)
    swap = pltpu.make_async_remote_copy(
        src_ref=grads.at[pl.ds(other * half, half)], dst_ref=pair_got, send_sem=psend.at[0],
        recv_sem=precv.at[0], device_id=partner, device_id_type=MESH)
    swap.start()
    swap.wait()
    half_sum[...] = (grads[pl.ds(core * half, half)] + pair_got[...]).reshape(half_sum.shape)

    def spot(peer):
        return (peer // width, 2 * lax.rem(peer, width) + core)

    def reduce_copy(slot, peer):
        return pltpu.make_async_remote_copy(
            src_ref=half_sum.at[jnp.minimum(peer, used - 1)], dst_ref=parts.at[slot],
            send_sem=rsend.at[peer], recv_sem=rrecv.at[slot], device_id=spot(peer),
            device_id_type=MESH)

    def gather_copy(chunk, peer):
        return pltpu.make_async_remote_copy(
            src_ref=mine, dst_ref=total_ref.at[core * used + jnp.minimum(chunk, used - 1)],
            send_sem=gsend.at[peer], recv_sem=grecv.at[chunk], device_id=spot(peer),
            device_id_type=MESH)

    def loop(body):
        def step(n, carry):
            body(lax.rem(chip + n, chips))
            return carry
        lax.fori_loop(1, chips, step, 0)

    def start_reduce(peer):
        @pl.when(peer < used)
        def _():
            reduce_copy(chip, peer).start()

    def end_reduce(peer):
        @pl.when(peer < used)
        def _():
            reduce_copy(chip, peer).wait_send()

        @pl.when(chip < used)
        def _():
            reduce_copy(peer, peer).wait_recv()

    def end_gather(peer):
        @pl.when(chip < used)
        def _():
            gather_copy(chip, peer).wait_send()

        @pl.when(peer < used)
        def _():
            gather_copy(peer, peer).wait_recv()

    loop(start_reduce)

    @pl.when(chip < used)
    def _():
        parts[chip] = half_sum[jnp.minimum(chip, used - 1)]

    loop(end_reduce)

    @pl.when(chip < used)
    def _():
        total = parts[0]
        for n in range(1, chips):
            total = total + parts[n]
        mine[...] = total
        total_ref[core * used + jnp.minimum(chip, used - 1)] = total
        loop(lambda peer: gather_copy(chip, peer).start())

    loop(end_gather)
    share = pltpu.make_async_remote_copy(
        src_ref=total_ref.at[pl.ds(core * used, used)],
        dst_ref=total_ref.at[pl.ds(core * used, used)],
        send_sem=psend.at[1], recv_sem=precv.at[1], device_id=partner, device_id_type=MESH)
    share.start()
    share.wait_send()
    pltpu.make_async_remote_copy(
        src_ref=total_ref.at[pl.ds(other * used, used)],
        dst_ref=total_ref.at[pl.ds(other * used, used)],
        send_sem=psend.at[1], recv_sem=precv.at[1], device_id=partner,
        device_id_type=MESH).wait_recv()


def last_kernel(code_ref, req_ref, slot_ref, gin_ref, plane_ref, ans_ref, arr_ref, order_ref,
                spread_ref, grad_ref, out_ref, fg_acc):
    fg_acc[...] = jnp.zeros_like(fg_acc)
    face_total = plane_ref.shape[0]

    def add_plane(n, carry):
        code = code_ref[n]

        @pl.when((code >= 0) & (code < face_total))
        def _():
            fg_acc[code] += plane_ref[n].astype(F32)
        return carry

    lax.fori_loop(0, face_total, add_plane, 0, unroll=4)
    for s in range(24):
        want = req_ref[s]

        @pl.when(want >= 0)
        def _():
            fg_acc[want] += ans_ref[s].astype(F32)

    out_ref[...] = jnp.zeros_like(out_ref)

    def put_block(s, carry):
        spot = slot_ref[s]

        @pl.when(spot >= 0)
        def _():
            out_ref[spot] = arr_ref[s]
        return carry

    lax.fori_loop(0, 64, put_block, 0)
    lane = lax.broadcasted_iota(jnp.int32, (32, LANES), 1)
    k_low = (lane % 128) < 64

    def split(v):
        high = v.astype(BF)
        return high, (v - high.astype(F32)).astype(BF)

    def one(b, carry):
        base = b * 6
        f = [fg_acc[base + n] for n in range(6)]
        j_sum = jnp.concatenate([f[2], f[3]], axis=1)
        k_sum = jnp.concatenate(
            [f[4][:, 0:64], f[5][:, 0:64], f[4][:, 64:128], f[5][:, 64:128]], axis=1)
        zero = jnp.zeros_like(k_sum)
        parts = split(j_sum) + split(jnp.where(k_low, k_sum, zero)) + split(
            jnp.where(k_low, zero, k_sum))
        stack = jnp.concatenate(parts, axis=0)
        spread = jnp.concatenate(
            [dot(spread_ref[0], stack[:, 0:128]), dot(spread_ref[1], stack[:, 128:256])], axis=1)
        total = gin_ref[pl.ds(b * ROWS, ROWS), :] + spread
        low = jnp.concatenate([f[0][0:16], f[0][16:32]], axis=1)
        high = jnp.concatenate([f[1][0:16], f[1][16:32]], axis=1)
        total = jnp.concatenate(
            [total[0:16] + low, total[16:112], total[112:128] + high], axis=0)
        turned = total.T.astype(BF)
        wide = jnp.concatenate([turned[q * 64:q * 64 + 64] for q in range(4)], axis=1)
        grad_ref[b] = dot(wide, order_ref[...]).astype(BF)
        return carry

    lax.fori_loop(0, grad_ref.shape[0], one, 0)


def on_device(features, fine_weight, down_weight, coarse_weight, cotangent, face_source,
              face_requests, child_slot, parent_octant):
    regions = lax.axis_size("region")
    owners = lax.axis_size("space")
    count = regions * owners
    bricks, channels, volume = features.shape
    faces = bricks * 6
    parents, _, wide = cotangent.shape
    octant = volume // 8
    slots = parent_octant.shape[1]
    shape = jax.ShapeDtypeStruct
    vm = pltpu.VMEM
    dma = pltpu.SemaphoreType.DMA
    codes = face_source.reshape(faces)
    requests = face_requests.reshape(24)
    targets = parent_octant.reshape(slots)
    child_inv, face_inv = pl.pallas_call(
        index_kernel,
        out_shape=(shape((slots,), jnp.int32), shape((24,), jnp.int32)),
        in_specs=[SMEM_SPEC] * 2,
        out_specs=(SMEM_SPEC,) * 2,
        name="index",
    )(codes, child_slot)
    scale_fine = 1.0 / math.sqrt(bricks * count * volume)
    scale_coarse = 1.0 / math.sqrt(parents * count * volume)
    chips = count // 2
    chunk = max(8, 448 // chips)
    used = 448 // chunk
    big = bricks * ROWS
    small = bricks * octant
    gin, planes, answers, arrived, totals = pl.pallas_call(
        functools.partial(main_kernel, regions, owners, scale_fine, scale_coarse),
        out_shape=(shape((big, LANES), F32), shape((faces, 32, 128), BF),
                   shape((6, 4, 32, 128), BF), shape((slots, octant, wide), BF),
                   shape((2 * used, chunk, 128), F32)),
        in_specs=[SMEM_SPEC] * 6 + [ANY_SPEC] * 3 + [VMEM_SPEC] * 4,
        out_specs=(VMEM_SPEC,) * 3 + (ANY_SPEC, VMEM_SPEC),
        scratch_shapes=[
            vm((bricks, channels, volume), BF), vm((slots, octant, wide), BF), vm((512, 512), BF),
            vm((big, LANES), BF), vm((faces, 32, 128), BF), vm((6, 4, 32, 128), BF),
            vm((6, 4, 32, 128), BF), vm((slots, octant, wide), BF), vm((slots, octant, wide), BF),
            vm((1280, LANES), BF), vm((1280, LANES), BF), vm((big, 1280), BF),
            vm((small, 512), BF), vm((big, LANES), BF), vm((small, wide), BF),
            vm((small, wide), BF), vm((small, wide), BF),
            vm((bricks, octant, wide), BF), vm((slots, octant, wide), BF), vm((big, LANES), F32),
            vm((small, wide), F32), vm((6, 4, 32, 128), BF), vm((2, ROWS, 128), F32),
            vm((2, ROWS, 128), F32), vm((112, 8, 128), F32), vm((56, 8, 128), F32),
            vm((used, chunk, 128), F32), vm((chips, chunk, 128), F32), vm((chunk, 128), F32),
            dma((3,)), dma((6,)), dma((6,)), dma((owners,)), dma((owners,)), dma((6,)), dma((6,)),
            dma((owners,)), dma((owners,)), dma, dma((2,)), dma((2,)), dma((chips,)),
            dma((chips,)), dma((chips,)), dma((chips,))],
        compiler_params=pltpu.CompilerParams(
            collective_id=0, has_side_effects=True, vmem_limit_bytes=60 * 2**20),
        name="main",
    )(codes, child_slot, requests, targets, child_inv, face_inv, features,
      cotangent.reshape(parents * 8, octant, wide), jnp.asarray(ORDER), jnp.asarray(FACE),
      fine_weight, down_weight.reshape(8 * channels, wide), coarse_weight)
    grad_in, coarse_out = pl.pallas_call(
        last_kernel,
        out_shape=(shape((bricks, channels, volume), BF), shape((parents * 8, octant, wide), BF)),
        in_specs=[SMEM_SPEC] * 3 + [VMEM_SPEC] * 6,
        out_specs=(VMEM_SPEC,) * 2,
        scratch_shapes=[vm((faces, 32, 128), F32)],
        compiler_params=pltpu.CompilerParams(vmem_limit_bytes=60 * 2**20),
        name="last",
    )(codes, requests, targets, gin, planes, answers.reshape(24, 32, 128), arrived,
      jnp.asarray(ORDER), jnp.asarray(SPREAD))
    totals = totals.reshape(896, 128)
    fine = totals[0:256].reshape(4, 64, 2, 64).transpose(0, 2, 1, 3).reshape(8, 64, 64)[0:7]
    return (grad_in, coarse_out.reshape(parents, volume, wide), fine,
            totals[256:768].reshape(8, channels, wide), totals[768:896])


def solution(mesh):
    both = ("region", "space")
    return jax.shard_map(
        on_device,
        mesh=mesh,
        in_specs=(P(both, None, None), P(), P(), P(), P(both, None, None), P(both, None),
                  P(both, None), P(both), P(both, None)),
        out_specs=(P(both, None, None), P(both, None, None), P(), P(), P()),
        check_vma=False,
    )
```

time: 123 us -> 81.4 us (0.66)
  Pallas kernels: 118 us -> 76.9 us
    pallas_call x4 -> x2, Pallas kernels: 105 us -> 63.5 us  [the longest x1 62.1 us: on_device(): pl.pallas_call(functools.partial(main_kernel, regions, owners, scale_fine...]
where the time goes in v1:
time: 81.4 us; the launch traced here: 81.2 us
  Pallas kernels  76.9 us (94%)
  local copies, waits for them, and re-layouts  3.64 us (4%)
    pallas_call x1, Pallas kernels, on_device(): pl.pallas_call(functools.partial(main_kernel, regions, owners, scale_fine...  62.1 us
    pallas_call x1, Pallas kernels, on_device(): pl.pallas_call(last_kernel, out_shape=(shape((bricks, channels, volume),...  13.4 us

profile of v1, /device:TPU:1, one launch (start us, length us, event | category | flops | bytes accessed | tf_op | source)
XLA Modules:
  0.0 81.2 jit_solution(14032880603137097901)
XLA Ops:
  0.6 0.8 copy.19
  1.4 0.6 reshape.46.code_ref
  2.0 1.4 %index.1 = (s32[64]{0:T(128)}, s32[24]{0:T(128)}) custom-call(s32[96]{0:T(128)} %reshape.46.code_ref, s32[16]{0:T(128)} %slot_ref.3), custom_call_target="tpu_custom_call" | custom-call | tf_op jit(solution)/shard_map/index/pallas_call | solution.py:628
  3.4 62.1 %main.1 = (f32[2048,256]{1,0:T(8,128)}, bf16[96,32,128]{2,1,0:T(8,128)(2,1)}, bf16[6,4,32,128]{3,2,1,0:T(8,128)(2,1)}, bf16[64,64,128]{2,1,0:T(8,128)(2,1)}, f32[112,8,128]{2,1,0:T(8,128)}) custom-call(s32[96]{0:T(128)} %reshape.46.code_ref, s32[16]{0:T(128)} %slot_ref.3, s32[24]{0:T(128)} %bitcast.17, s32[64]{0:T(128)} %bitcast.19, ...), custom_call_target="tpu_custom_call" | custom-call | tf_op jit(solution)/shard_map/main/pallas_call | solution.py:642
  65.5 0.0 copy-start
  65.5 13.4 %last.1 = (bf16[16,64,512]{2,1,0:T(8,128)(2,1)}, bf16[64,64,128]{2,1,0:T(8,128)(2,1)}) custom-call(s32[96]{0:T(128)} %reshape.46.code_ref, s32[24]{0:T(128)} %bitcast.18, s32[64]{0:T(128)} %bitcast.20, f32[2048,256]{1,0:T(8,128)} %get-tuple-element.16.gin_ref, bf16[96,32,128]{2,1,0:T(8,128)(2,1)} %get-tuple-element.17.plane_ref, ...), custom_call_target="tpu_custom_call" | custom-call | tf_op jit(solution)/shard_map/last/pallas_call | solution.py:669
  78.9 0.0 copy-done
  78.9 0.6 slice_bitcast_fusion
  79.6 0.7 slice.19
  80.3 0.2 reshape.53
  80.5 0.7 slice.22
  (2 shorter events, 0.0 us)
Async XLA Ops:
  65.5 13.4 %copy-start = (f32[112,8,128]{2,1,0:T(8,128)S(1)}, f32[112,8,128]{2,1,0:T(8,128)}, u32[]{:S(2)}) copy-start(f32[112,8,128]{2,1,0:T(8,128)} %get-tuple-element.22) | copy-start | bytes 1376260

commit v2 on v1

v2 whole, which is shorter than its diff:
```python
import functools
import math

import jax
import jax.numpy as jnp
import numpy as np
from jax import lax
from jax.experimental import pallas as pl
from jax.experimental.pallas import tpu as pltpu
from jax.sharding import PartitionSpec as P

EDGE = 8
BF = jnp.bfloat16
F32 = jnp.float32
MESH = pl.DeviceIdType.MESH
NT = (((1,), (1,)), ((), ()))
TN = (((0,), (0,)), ((), ()))
VMEM_SPEC = pl.BlockSpec(memory_space=pltpu.VMEM)
SMEM_SPEC = pl.BlockSpec(memory_space=pltpu.SMEM)
ANY_SPEC = pl.BlockSpec(memory_space=pl.ANY)
ROWS = 128
LANES = 256
GROUP = 4


def row_of(i, j, k):
    return i * 16 + j * 4 + k


def make_tables():
    order = np.zeros((512, 512), np.float32)
    for i in range(8):
        for j in range(8):
            for k in range(8):
                q = (j % 2) * 2 + k % 2
                order[q * 128 + row_of(i, j // 2, k // 2), i * 64 + j * 8 + k] = 1
    face = np.zeros((128, 128), np.float32)
    for i in range(8):
        for m in range(4):
            face[i * 4 + m, row_of(i, 0, m)] = 1
            face[32 + i * 4 + m, row_of(i, 3, m)] = 1
            face[64 + i * 4 + m, row_of(i, m, 0)] = 1
            face[96 + i * 4 + m, row_of(i, m, 3)] = 1
    cast = lambda a: np.asarray(a, dtype=BF)
    return cast(order), cast(order.T), cast(face)


ORDER, ORDER_T, FACE = make_tables()


def dot(a, b, dims=(((1,), (0,)), ((), ()))):
    return lax.dot_general(a, b, dims, preferred_element_type=F32)


def neighbours(regions, owners):
    far = owners // 4
    return [(1, 0), (-1, 0), (0, 1), (0, -1), (0, far), (0, -far)]


def face_moves(regions, owners, my_r, my_s, backward):
    sign = -1 if backward else 1
    for k, (dr, ds) in enumerate(neighbours(regions, owners)):
        to_r, to_s = my_r + sign * dr, my_s + sign * ds
        from_r, from_s = my_r - sign * dr, my_s - sign * ds
        can_send = (to_r >= 0) & (to_r < regions) & (to_s >= 0) & (to_s < owners)
        can_take = (from_r >= 0) & (from_r < regions) & (from_s >= 0) & (from_s < owners)
        yield k, (to_r, to_s), can_send, can_take


def send_faces(regions, owners, my_r, my_s, backward, src, dst, send_sem, recv_sem):
    for k, target, can_send, can_take in face_moves(regions, owners, my_r, my_s, backward):
        copy = pltpu.make_async_remote_copy(
            src_ref=src.at[k], dst_ref=dst.at[k], send_sem=send_sem.at[k],
            recv_sem=recv_sem.at[k], device_id=target, device_id_type=MESH)

        @pl.when(can_send)
        def _():
            copy.start()


def wait_faces(regions, owners, my_r, my_s, backward, src, dst, send_sem, recv_sem):
    for k, target, can_send, can_take in face_moves(regions, owners, my_r, my_s, backward):
        copy = pltpu.make_async_remote_copy(
            src_ref=src.at[k], dst_ref=dst.at[k], send_sem=send_sem.at[k],
            recv_sem=recv_sem.at[k], device_id=target, device_id_type=MESH)

        @pl.when(can_send)
        def _():
            copy.wait_send()

        @pl.when(can_take)
        def _():
            copy.wait_recv()


def block_copy(my_r, peer, pair, take, land, src, dst, send_sem, recv_sem):
    return pltpu.make_async_remote_copy(
        src_ref=src.at[pl.ds(take * pair, pair)], dst_ref=dst.at[pl.ds(land * pair, pair)],
        send_sem=send_sem, recv_sem=recv_sem, device_id=(my_r, peer),
        device_id_type=MESH)


def start_blocks(owners, my_r, my_s, pair, src, dst, send_sem, recv_sem):
    def start(step, carry):
        peer = lax.rem(my_s + step, owners)
        block_copy(my_r, peer, pair, peer, my_s, src, dst, send_sem, recv_sem).start()
        return carry

    lax.fori_loop(1, owners, start, 0)


def wait_blocks(owners, my_r, my_s, pair, src, dst, send_sem, recv_sem):
    count = (owners - 1) * pair
    copy = pltpu.make_async_remote_copy(
        src_ref=src.at[pl.ds(0, count)], dst_ref=dst.at[pl.ds(0, count)], send_sem=send_sem,
        recv_sem=recv_sem, device_id=(my_r, lax.rem(my_s + 1, owners)), device_id_type=MESH)
    copy.wait_send()
    copy.wait_recv()


def silu_parts(v):
    s = 1.0 / (1.0 + jnp.exp(-v))
    return v * s, s * (1.0 + v * (1.0 - s))


def place(w_ref, base, q_in, q_out, block):
    w_ref[base + q_in * 64:base + q_in * 64 + 64, q_out * 64:q_out * 64 + 64] = block


SWAP = (0, 2, 1, 3)


def fill_weights(fine_ref, w_ref, wt_ref):
    w_ref[...] = jnp.zeros_like(w_ref)
    wt_ref[...] = jnp.zeros_like(wt_ref)
    same = [(q, q) for q in range(4)]
    up_j = [(0, 2), (1, 3)]
    down_j = [(2, 0), (3, 1)]
    up_k = [(0, 1), (2, 3)]
    down_k = [(1, 0), (3, 2)]
    plan = [
        (0, 0, 0, same), (1, 1, 2, same), (2, 2, 1, same),
        (3, 0, 0, up_j), (3, 3, 3, down_j), (4, 0, 0, down_j), (4, 3, 3, up_j),
        (5, 0, 0, up_k), (5, 4, 4, down_k), (6, 0, 0, down_k), (6, 4, 4, up_k),
    ]
    for tap, fwd, bwd, pairs in plan:
        w = fine_ref[tap]
        wt = w.astype(F32).T.astype(BF)
        for q_in, q_out in pairs:
            place(w_ref, fwd * 256, SWAP[q_in] if fwd == 4 else q_in, q_out, w)
            place(wt_ref, bwd * 256, SWAP[q_out] if bwd == 4 else q_out, q_in, wt)
    return plan


def index_kernel(code_ref, slot_ref, req_ref, child_ref, face_ref, prev_ref, last_ref):
    total = code_ref.shape[0]
    none = prev_ref.shape[0]
    for s in range(child_ref.shape[0]):
        child_ref[s] = 0
    for s in range(face_ref.shape[0]):
        face_ref[s] = 0
    for f in range(total):
        last_ref[f] = none
    for b in range(slot_ref.shape[0]):
        child_ref[slot_ref[b]] = b

    def mark(n, carry):
        code = code_ref[n]

        @pl.when(code >= total)
        def _():
            face_ref[code - total] = n

        @pl.when((code >= 0) & (code < total))
        def _():
            prev_ref[n] = last_ref[code]
            last_ref[code] = n

        @pl.when((code < 0) | (code >= total))
        def _():
            prev_ref[n] = none
        return carry

    lax.fori_loop(0, total, mark, 0)

    def answer(s, carry):
        want = req_ref[s]

        @pl.when(want >= 0)
        def _():
            prev_ref[total + s] = last_ref[want]
            last_ref[want] = total + s

        @pl.when(want < 0)
        def _():
            prev_ref[total + s] = none
        return carry

    lax.fori_loop(0, req_ref.shape[0], answer, 0)


def signal_peers(regions, owners, my_r, my_s):
    barrier = pltpu.get_barrier_semaphore()

    def greet(step, carry):
        peer = lax.rem(my_s + step, owners)
        pl.semaphore_signal(barrier, inc=1, device_id=(my_r, peer), device_id_type=MESH)
        return carry

    lax.fori_loop(1, owners, greet, 0)

    for step in range(1, regions):
        far_r = lax.rem(my_r + step, regions)
        pl.semaphore_signal(barrier, inc=1, device_id=(far_r, my_s), device_id_type=MESH)


def wait_peers(regions, owners):
    barrier = pltpu.get_barrier_semaphore()
    pl.semaphore_wait(barrier, owners - 1 + regions - 1)


def row_roll(v, by):
    return pltpu.roll(v, by % v.shape[0], 0)


def pieces8(v, start, step, count):
    return jnp.concatenate([v[start + n * step:start + n * step + 8] for n in range(count)], axis=0)


def main_kernel(regions, owners, scale_fine, scale_coarse,
                code_ref, slot_ref, req_ref, po_ref, child_inv, face_inv, prev_ref, last_ref,
                feat_hbm, cot_hbm, order_t_hbm, order_hbm, face_ref, fine_ref, down_ref,
                coarse_ref,
                grad_ref, blocks_out, total_ref,
                feat, cot, order_t, order, x_ref, xk_ref, table, out_face, in_face, cots,
                got_cots, w_ref, wt_ref, taps_ref, act_ref, gh_ref, red_ref, cg_ref, ch_ref,
                co_ref, co_slots, slope_ref, cslope_ref, gin_ref, plane_ref, back_face, ans_ref,
                chain, halo_scr, g_scr,
                grads, pair_got, half_sum, part_x, x_sum, part_p, mine,
                load, fsend, frecv, hsend, hrecv, osem, bsem, csem, rsem):
    my_r = lax.axis_index("region")
    my_s = lax.axis_index("space")
    bricks = feat.shape[0]
    face_total = table.shape[0]
    slots = cots.shape[0]
    pair = slots // owners
    groups = bricks // GROUP
    wide_rows = GROUP * ROWS
    half_rows = GROUP * 64
    loads = [pltpu.make_async_copy(src, dst, load.at[n]) for n, (src, dst) in enumerate(
        [(feat_hbm, feat), (order_t_hbm, order_t), (cot_hbm, cot), (order_hbm, order)])]
    for copy in loads:
        copy.start()
    signal_peers(regions, owners, my_r, my_s)
    loads[2].wait()

    def gather_cot(s, carry):
        cots[s] = cot[jnp.maximum(po_ref[s], 0)]
        return carry

    lax.fori_loop(0, slots, gather_cot, 0, unroll=8)
    loads[0].wait()
    loads[1].wait()

    def turn(g, carry):
        block = feat[pl.ds(g * GROUP, GROUP)].reshape(half_rows, 512)
        moved = dot(block, order_t[...]).astype(BF)
        for n in range(GROUP):
            b = g * GROUP + n
            row = pl.multiple_of(b * ROWS, ROWS)
            part = moved[n * 64:(n + 1) * 64]
            q = [part[:, m * 128:(m + 1) * 128] for m in range(4)]
            x = jnp.concatenate(q, axis=0).T
            x_ref[pl.ds(row, ROWS), :] = x
            xk = jnp.concatenate([q[m] for m in SWAP], axis=0).T
            xk_ref[pl.ds(row, ROWS), :] = xk
            fj = dot(face_ref[0:64], x).astype(BF)
            fk = dot(face_ref[64:128], xk).astype(BF)
            base = b * 6
            table[base] = jnp.concatenate([x[0:16, 0:128], x[0:16, 128:256]], axis=0)
            table[base + 1] = jnp.concatenate([x[112:128, 0:128], x[112:128, 128:256]], axis=0)
            table[base + 2] = fj[0:32, 0:128]
            table[base + 3] = fj[32:64, 128:256]
            table[base + 4] = fk[0:32, 0:128]
            table[base + 5] = fk[32:64, 128:256]
        return carry

    lax.fori_loop(0, groups, turn, 0)
    for s in range(24):
        out_face[s // 4, s % 4] = table[jnp.maximum(req_ref[s], 0)]
    wait_peers(regions, owners)
    send_faces(regions, owners, my_r, my_s, False, out_face, in_face, fsend, frecv)
    start_blocks(owners, my_r, my_s, pair, cots, got_cots, bsem.at[0], bsem.at[1])
    plan = fill_weights(fine_ref, w_ref, wt_ref)
    wait_faces(regions, owners, my_r, my_s, False, out_face, in_face, fsend, frecv)

    row8 = lax.broadcasted_iota(jnp.int32, (ROWS, 128), 0)
    first_j = lax.rem(row8, 16) < 4
    last_j = lax.rem(row8, 16) >= 12
    first_k = lax.rem(row8, 4) == 0
    last_k = lax.rem(row8, 4) == 3
    low4 = lax.rem(lax.broadcasted_iota(jnp.int32, (32, 128), 0), 8) < 4

    def halo(b, d):
        code = code_ref[b * 6 + d]
        own = table[jnp.clip(code, 0, face_total - 1)]
        slot = jnp.clip(code - face_total, 0, 23)
        got = in_face[slot // 4, lax.rem(slot, 4)]
        picked = jnp.where(code >= face_total, got, own)
        return jnp.where(code >= 0, picked, jnp.zeros_like(picked))

    def spread_j(slab, to_last):
        if to_last:
            even, odd = row_roll(slab, 4), slab
        else:
            even, odd = slab, row_roll(slab, -4)
        rows = []
        for i in range(8):
            piece = (even if i % 2 == 0 else odd)[(i // 2) * 8:(i // 2) * 8 + 8]
            rows += [piece, piece]
        return jnp.concatenate(rows, axis=0)

    def pick_j(values, from_last):
        if from_last:
            return jnp.where(low4, row_roll(pieces8(values, 8, 32, 4), -4),
                             pieces8(values, 24, 32, 4))
        return jnp.where(low4, pieces8(values, 0, 32, 4),
                         row_roll(pieces8(values, 16, 32, 4), 4))

    def forward_taps(b, n):
        row = pl.multiple_of(b * ROWS, ROWS)
        x = x_ref[pl.ds(row, ROWS), :]
        xk = xk_ref[pl.ds(row, ROWS), :].astype(F32)
        x32 = x.astype(F32)
        h = [halo(b, d) for d in range(6)]
        halo_scr[n, pl.ds(3, 32, stride=4), :] = h[5].astype(F32)
        halo_scr[n, pl.ds(0, 32, stride=4), :] = h[4].astype(F32)
        edge = halo_scr[n]
        out = pl.ds(row, ROWS)
        taps_ref[out, 0:256] = x
        taps_ref[out, 256:512] = jnp.concatenate(
            [jnp.concatenate([h[0][0:16], h[0][16:32]], axis=1), x[0:112]], axis=0)
        taps_ref[out, 512:768] = jnp.concatenate(
            [x[16:128], jnp.concatenate([h[1][0:16], h[1][16:32]], axis=1)], axis=0)
        taps_ref[out, 768:896] = jnp.where(
            last_j, spread_j(h[3].astype(F32), True), row_roll(x32[:, 0:128], -4)).astype(BF)
        taps_ref[out, 896:1024] = jnp.where(
            first_j, spread_j(h[2].astype(F32), False), row_roll(x32[:, 128:256], 4)).astype(BF)
        taps_ref[out, 1024:1152] = jnp.where(
            last_k, edge, row_roll(xk[:, 0:128], -1)).astype(BF)
        taps_ref[out, 1152:1280] = jnp.where(
            first_k, edge, row_roll(xk[:, 128:256], 1)).astype(BF)

    def forward(g, carry):
        for n in range(GROUP):
            forward_taps(g * GROUP + n, n)
        row = pl.multiple_of(g * wide_rows, wide_rows)
        half = pl.multiple_of(g * half_rows, half_rows)
        for n in range(GROUP):
            part = pl.ds(pl.multiple_of(row + n * ROWS, ROWS), ROWS)
            hidden = dot(taps_ref[part, :], w_ref[...])
            act, slope = silu_parts(hidden)
            slope_ref[part, :] = slope
            act = act.astype(BF)
            dst = pl.ds(pl.multiple_of(half + n * 64, 64), 64)
            act_ref[dst, 0:256] = jnp.concatenate(
                [act[32 * m:32 * m + 16] for m in range(4)], axis=0)
            act_ref[dst, 256:512] = jnp.concatenate(
                [act[32 * m + 16:32 * m + 32] for m in range(4)], axis=0)
        out = pl.ds(half, half_rows)
        reduced = dot(act_ref[out, :], down_ref[...]).astype(BF)
        red_ref[out, :] = reduced
        c_out, c_slope = silu_parts(dot(reduced, coarse_ref[...]))
        co_ref[pl.ds(g * GROUP, GROUP)] = c_out.astype(BF).reshape(GROUP, 64, 128)
        cslope_ref[out, :] = c_slope
        return carry

    lax.fori_loop(0, groups, forward, 0)

    def gather_out(s, carry):
        co_slots[s] = co_ref[child_inv[s]]
        return carry

    lax.fori_loop(0, slots, gather_out, 0, unroll=8)
    wait_blocks(owners, my_r, my_s, pair, cots, got_cots, bsem.at[0], bsem.at[1])
    for u in range(pair):
        got_cots[my_s * pair + u] = cots[my_s * pair + u]
    start_blocks(owners, my_r, my_s, pair, co_slots, blocks_out, csem.at[0], csem.at[1])
    keep = pltpu.make_async_copy(co_slots.at[pl.ds(my_s * pair, pair)],
                                 blocks_out.at[pl.ds(my_s * pair, pair)], osem)
    keep.start()

    def coarse_back(g, carry):
        row = pl.multiple_of(g * wide_rows, wide_rows)
        half = pl.multiple_of(g * half_rows, half_rows)
        out = pl.ds(half, half_rows)
        cot_rows = jnp.concatenate(
            [got_cots[slot_ref[g * GROUP + n]] for n in range(GROUP)], axis=0).astype(F32)
        c_grad = (cot_rows * cslope_ref[out, :]).astype(BF)
        cg_ref[out, :] = c_grad
        child = dot(c_grad, coarse_ref[...], NT).astype(BF)
        ch_ref[out, :] = child
        ga = dot(child, down_ref[...], NT)
        for n in range(GROUP * 4):
            for a in range(2):
                part = pl.ds(pl.multiple_of(row + n * 32 + a * 16, 16), 16)
                gh_ref[part, :] = (ga[16 * n:16 * n + 16, a * 256:a * 256 + 256]
                                   * slope_ref[part, :]).astype(BF)
        return carry

    lax.fori_loop(0, groups, coarse_back, 0)

    def put_rows(start, value):
        count = value.shape[0] // 8
        grads[start // 8:start // 8 + count] = value.reshape(count, 8, 128)

    turned = dot(gh_ref[...], taps_ref[...], TN) * scale_fine
    sums = [None] * 7
    for tap, fwd, bwd, pairs in plan:
        for q_in, q_out in pairs:
            spot = fwd * 256 + (SWAP[q_in] if fwd == 4 else q_in) * 64
            part = turned[q_out * 64:q_out * 64 + 64, spot:spot + 64]
            sums[tap] = part if sums[tap] is None else sums[tap] + part
    sums.append(jnp.zeros_like(sums[0]))
    for n in range(4):
        put_rows(n * 64, jnp.concatenate([sums[2 * n], sums[2 * n + 1]], axis=0).T)
    put_rows(256, dot(act_ref[...], ch_ref[...], TN) * scale_fine)
    put_rows(768, dot(red_ref[...], cg_ref[...], TN) * scale_coarse)
    phases = sum_phases(regions, owners, my_r, my_s, grads, pair_got, half_sum, part_x, x_sum,
                        part_p, mine, total_ref, rsem)
    next(phases)

    def backward(g):
        row = g * wide_rows
        bwd, f0, f1, fj, fk = [], [], [], [], []
        for n in range(GROUP):
            gh = gh_ref[row + n * ROWS:row + (n + 1) * ROWS, :]
            g32 = gh.astype(F32)
            low, high = g32[:, 0:128], g32[:, 128:256]
            zero = jnp.zeros_like(low)
            swapped = jnp.concatenate([gh[:, 0:64], gh[:, 128:192], gh[:, 64:128], gh[:, 192:256]],
                                      axis=1).astype(F32)
            k_low, k_high = swapped[:, 0:128], swapped[:, 128:256]
            blank = jnp.zeros((16, LANES), BF)
            bwd.append(jnp.concatenate([
                gh,
                jnp.concatenate([blank, gh[0:112]], axis=0),
                jnp.concatenate([gh[16:128], blank], axis=0),
                jnp.where(last_j, zero, row_roll(low, -4)).astype(BF),
                jnp.where(first_j, zero, row_roll(high, 4)).astype(BF),
                jnp.where(last_k, zero, row_roll(k_low, -1)).astype(BF),
                jnp.where(first_k, zero, row_roll(k_high, 1)).astype(BF)], axis=1))
            f0.append(gh[0:16])
            f1.append(gh[112:128])
            fj.append(jnp.concatenate([pick_j(low, False), pick_j(high, True)], axis=1).astype(BF))
            g_scr[2 * n] = k_low
            g_scr[2 * n + 1] = k_high
            fk.append(jnp.concatenate([g_scr[2 * n, pl.ds(0, 32, stride=4), :],
                                       g_scr[2 * n + 1, pl.ds(3, 32, stride=4), :]],
                                      axis=1).astype(BF))
        for n in range(GROUP):
            gin_ref[row + n * ROWS:row + (n + 1) * ROWS, :] = dot(bwd[n], wt_ref[...])
        p0 = dot(jnp.concatenate(f0, axis=0), wt_ref[512:768, :]).astype(BF)
        p1 = dot(jnp.concatenate(f1, axis=0), wt_ref[256:512, :]).astype(BF)
        pj = dot(jnp.concatenate(fj, axis=0), wt_ref[768:1024, :]).astype(BF)
        pk = dot(jnp.concatenate(fk, axis=0), wt_ref[1024:1280, :]).astype(BF)
        for n in range(GROUP):
            base = (g * GROUP + n) * 6
            a, c = p0[n * 16:n * 16 + 16], p1[n * 16:n * 16 + 16]
            j, k = pj[n * 32:n * 32 + 32], pk[n * 32:n * 32 + 32]
            plane_ref[base] = jnp.concatenate([a[:, 0:128], a[:, 128:256]], axis=0)
            plane_ref[base + 1] = jnp.concatenate([c[:, 0:128], c[:, 128:256]], axis=0)
            plane_ref[base + 2] = j[:, 128:256]
            plane_ref[base + 3] = j[:, 0:128]
            plane_ref[base + 4] = jnp.concatenate([k[:, 64:128], k[:, 192:256]], axis=1)
            plane_ref[base + 5] = jnp.concatenate([k[:, 0:64], k[:, 128:192]], axis=1)

    for g in range(groups):
        backward(g)
        if g == 0 or g == 2:
            next(phases)
    for s in range(24):
        back_face[s // 4, s % 4] = plane_ref[face_inv[s]]
    chain[face_total + 24] = jnp.zeros((32, 128), F32)
    send_faces(regions, owners, my_r, my_s, True, back_face, ans_ref, hsend, hrecv)

    def add_plane(n, carry):
        chain[n] = chain[prev_ref[n]] + plane_ref[n].astype(F32)
        return carry

    lax.fori_loop(0, face_total, add_plane, 0, unroll=4)
    next(phases)
    wait_faces(regions, owners, my_r, my_s, True, back_face, ans_ref, hsend, hrecv)
    for s in range(24):
        chain[face_total + s] = (chain[prev_ref[face_total + s]]
                                 + ans_ref[s // 4, s % 4].astype(F32))
    loads[3].wait()
    lane = lax.broadcasted_iota(jnp.int32, (ROWS, LANES), 1)
    edge_k = lax.rem(lax.broadcasted_iota(jnp.int32, (ROWS, LANES), 0), 4) == jnp.where(
        lax.rem(lane, 128) < 64, 0, 3)

    def finish(g, carry):
        wides = []
        for n in range(GROUP):
            b = g * GROUP + n
            f = [chain[last_ref[b * 6 + d]] for d in range(6)]
            zero = jnp.zeros((ROWS, 128), F32)
            add_j = jnp.concatenate([jnp.where(first_j, spread_j(f[2], False), zero),
                                     jnp.where(last_j, spread_j(f[3], True), zero)], axis=1)
            for side in range(2):
                k0 = f[4] if side == 0 else pltpu.roll(f[4], 64, 1)
                k3 = f[5] if side == 1 else pltpu.roll(f[5], 64, 1)
                g_scr[2 * n + side, pl.ds(0, 32, stride=4), :] = k0
                g_scr[2 * n + side, pl.ds(3, 32, stride=4), :] = k3
            add_k = jnp.where(edge_k, jnp.concatenate([g_scr[2 * n], g_scr[2 * n + 1]], axis=1),
                              jnp.zeros((ROWS, LANES), F32))
            total = gin_ref[pl.ds(pl.multiple_of(b * ROWS, ROWS), ROWS), :] + add_j + add_k
            low = jnp.concatenate([f[0][0:16], f[0][16:32]], axis=1)
            high = jnp.concatenate([f[1][0:16], f[1][16:32]], axis=1)
            total = jnp.concatenate(
                [total[0:16] + low, total[16:112], total[112:128] + high], axis=0).astype(BF)
            flipped = total.T
            wides.append(jnp.concatenate([flipped[q * 64:q * 64 + 64] for q in range(4)], axis=1))
        out = dot(jnp.concatenate(wides, axis=0), order[...]).astype(BF)
        grad_ref[pl.ds(g * GROUP, GROUP)] = out.reshape(GROUP, 64, 512)
        return carry

    lax.fori_loop(0, groups, finish, 0)
    for _ in phases:
        pass
    keep.wait()
    wait_blocks(owners, my_r, my_s, pair, co_slots, blocks_out, csem.at[0], csem.at[1])


def sum_phases(regions, owners, my_r, my_s, grads, pair_got, half_sum, part_x, x_sum, part_p, mine,
               total_ref, sem):
    core = lax.rem(my_s, 2)
    other = 1 - core
    place_ = my_s // 2
    places = owners // 2
    half = pair_got.shape[0]
    per_r = half // regions
    unit = mine.shape[0]
    used = per_r // unit
    partner = (my_r, my_s + 1 - 2 * core)

    def remote(src, dst, n, target):
        return pltpu.make_async_remote_copy(
            src_ref=src, dst_ref=dst, send_sem=sem.at[2 * n], recv_sem=sem.at[2 * n + 1],
            device_id=target, device_id_type=MESH)

    swap = remote(grads.at[pl.ds(other * half, half)], pair_got, 0, partner)
    swap.start()
    yield
    swap.wait()
    half_sum[...] = grads[pl.ds(core * half, half)] + pair_got[...]
    for n in range(1, regions):
        peer = lax.rem(my_r + n, regions)
        remote(half_sum.at[pl.ds(peer * per_r, per_r)], part_x.at[pl.ds(my_r * per_r, per_r)], 1,
               (peer, my_s)).start()
    yield
    far = (lax.rem(my_r + 1, regions), my_s)
    got = pl.ds(0, (regions - 1) * per_r)
    arrived = remote(half_sum.at[got], part_x.at[got], 1, far)
    arrived.wait_send()
    arrived.wait_recv()
    run = half_sum[pl.ds(my_r * per_r, per_r)]
    for n in range(1, regions):
        run = run + part_x[pl.ds(lax.rem(my_r + n, regions) * per_r, per_r)]
    x_sum[...] = run

    def spot(peer):
        return (my_r, 2 * peer + core)

    owns = place_ < used
    mine_at = jnp.minimum(place_, used - 1) * unit

    def start_sum(n, carry):
        peer = lax.rem(place_ + n, places)

        @pl.when(peer < used)
        def _():
            remote(x_sum.at[pl.ds(jnp.minimum(peer, used - 1) * unit, unit)],
                   part_p.at[pl.ds(place_ * unit, unit)], 2, spot(peer)).start()
        return carry

    lax.fori_loop(1, places, start_sum, 0)
    yield
    near = spot(lax.rem(place_ + 1, places))
    base = core * half + my_r * per_r
    out_at = base + mine_at

    def wait_sent(count, n, src):
        if count:
            remote(src.at[pl.ds(0, count * unit)], part_p.at[pl.ds(0, count * unit)], n,
                   near).wait_send()

    def wait_got(count, n, dst):
        if count:
            remote(dst.at[pl.ds(0, count * unit)], dst.at[pl.ds(0, count * unit)], n,
                   near).wait_recv()

    @pl.when(owns)
    def _():
        wait_sent(used - 1, 2, x_sum)
        wait_got(places - 1, 2, part_p)
        run = x_sum[pl.ds(mine_at, unit)]
        for n in range(1, places):
            run = run + part_p[pl.ds(lax.rem(place_ + n, places) * unit, unit)]
        mine[...] = run
        total_ref[pl.ds(out_at, unit)] = run

        def start_share(n, carry):
            remote(mine, total_ref.at[pl.ds(out_at, unit)], 3,
                   spot(lax.rem(place_ + n, places))).start()
            return carry

        lax.fori_loop(1, places, start_share, 0)

    @pl.when(jnp.logical_not(owns))
    def _():
        wait_sent(used, 2, x_sum)
    yield

    @pl.when(owns)
    def _():
        wait_sent(places - 1, 3, part_p)
        wait_got(used - 1, 3, total_ref)

    @pl.when(jnp.logical_not(owns))
    def _():
        wait_got(used, 3, total_ref)

    for n in range(1, regions):
        peer = lax.rem(my_r + n, regions)
        remote(total_ref.at[pl.ds(base, per_r)], total_ref.at[pl.ds(base, per_r)], 4,
               (peer, my_s)).start()
    yield
    gone = remote(total_ref.at[got], total_ref.at[got], 4, far)
    gone.wait_send()
    gone.wait_recv()
    own = pl.ds(core * half, half)
    remote(total_ref.at[own], total_ref.at[own], 5, partner).start()
    yield
    last = remote(total_ref.at[own], total_ref.at[pl.ds(other * half, half)], 5, partner)
    last.wait_send()
    last.wait_recv()


def result_kernel(slot_ref, made_ref, arr_ref, total_ref, grad_ref, out_ref, fine_ref, down_ref,
                  coarse_ref):
    out_ref[...] = jnp.zeros_like(out_ref)

    def put_block(s, carry):
        spot = slot_ref[s]

        @pl.when(spot >= 0)
        def _():
            out_ref[spot] = arr_ref[s]
        return carry

    lax.fori_loop(0, arr_ref.shape[0], put_block, 0, unroll=4)
    grad_ref[...] = made_ref[...]
    for tap in range(7):
        rows = total_ref[tap // 2 * 8:tap // 2 * 8 + 8].reshape(64, 128)
        fine_ref[tap] = rows[:, tap % 2 * 64:tap % 2 * 64 + 64]
    down_ref[...] = total_ref[32:96].reshape(512, 128)
    coarse_ref[...] = total_ref[96:112].reshape(128, 128)


def on_device(features, fine_weight, down_weight, coarse_weight, cotangent, face_source,
              face_requests, child_slot, parent_octant):
    regions = lax.axis_size("region")
    owners = lax.axis_size("space")
    count = regions * owners
    bricks, channels, volume = features.shape
    faces = bricks * 6
    parents, _, wide = cotangent.shape
    octant = volume // 8
    slots = parent_octant.shape[1]
    shape = jax.ShapeDtypeStruct
    vm = pltpu.VMEM
    dma = pltpu.SemaphoreType.DMA
    codes = face_source.reshape(faces)
    requests = face_requests.reshape(24)
    targets = parent_octant.reshape(slots)
    child_inv, face_inv, prev, last = pl.pallas_call(
        index_kernel,
        out_shape=(shape((slots,), jnp.int32), shape((24,), jnp.int32),
                   shape((faces + 24,), jnp.int32), shape((faces,), jnp.int32)),
        in_specs=[SMEM_SPEC] * 3,
        out_specs=(SMEM_SPEC,) * 4,
        name="index",
    )(codes, child_slot, requests)
    scale_fine = 1.0 / math.sqrt(bricks * count * volume)
    scale_coarse = 1.0 / math.sqrt(parents * count * volume)
    places = owners // 2
    per_r = 56 // regions
    unit = max(1, per_r // places)
    big = bricks * ROWS
    small = bricks * octant
    block = (slots, octant, wide)
    faces4 = (6, 4, 32, 128)
    made, arrived, totals = pl.pallas_call(
        functools.partial(main_kernel, regions, owners, scale_fine, scale_coarse),
        out_shape=(shape((bricks, channels, volume), BF), shape(block, BF),
                   shape((112, 8, 128), F32)),
        in_specs=[SMEM_SPEC] * 8 + [ANY_SPEC] * 4 + [VMEM_SPEC] * 4,
        out_specs=(VMEM_SPEC, ANY_SPEC, VMEM_SPEC),
        scratch_shapes=[
            vm((bricks, channels, volume), BF), vm(block, BF), vm((512, 512), BF),
            vm((512, 512), BF), vm((big, LANES), BF), vm((big, LANES), BF),
            vm((faces, 32, 128), BF), vm(faces4, BF), vm(faces4, BF), vm(block, BF), vm(block, BF),
            vm((1280, LANES), BF), vm((1280, LANES), BF), vm((big, 1280), BF),
            vm((small, 512), BF), vm((big, LANES), BF), vm((small, wide), BF),
            vm((small, wide), BF), vm((small, wide), BF),
            vm((bricks, octant, wide), BF), vm(block, BF), vm((big, LANES), F32),
            vm((small, wide), F32), vm((big, LANES), F32), vm((faces, 32, 128), BF),
            vm(faces4, BF), vm(faces4, BF), vm((faces + 25, 32, 128), F32),
            vm((GROUP, ROWS, 128), F32), vm((2 * GROUP, ROWS, 128), F32),
            vm((112, 8, 128), F32), vm((56, 8, 128), F32), vm((56, 8, 128), F32),
            vm((56, 8, 128), F32), vm((per_r, 8, 128), F32), vm((places * unit, 8, 128), F32),
            vm((unit, 8, 128), F32),
            dma((4,)), dma((6,)), dma((6,)), dma((6,)), dma((6,)), dma, dma((2,)), dma((2,)),
            dma((12,))],
        compiler_params=pltpu.CompilerParams(
            collective_id=0, has_side_effects=True, vmem_limit_bytes=60 * 2**20),
        name="main",
    )(codes, child_slot, requests, targets, child_inv, face_inv, prev, last, features,
      cotangent.reshape(parents * 8, octant, wide), jnp.asarray(ORDER_T), jnp.asarray(ORDER),
      jnp.asarray(FACE), fine_weight, down_weight.reshape(8 * channels, wide), coarse_weight)
    grad_in, coarse_out, fine, down, coarse = pl.pallas_call(
        result_kernel,
        out_shape=(shape((bricks, channels, volume), BF), shape((parents * 8, octant, wide), BF),
                   shape((7, channels, channels), F32), shape((8 * channels, wide), F32),
                   shape((wide, wide), F32)),
        in_specs=[SMEM_SPEC] + [VMEM_SPEC] * 3,
        out_specs=(VMEM_SPEC,) * 5,
        compiler_params=pltpu.CompilerParams(vmem_limit_bytes=60 * 2**20),
        name="result",
    )(targets, made, arrived, totals)
    return (grad_in, coarse_out.reshape(parents, volume, wide), fine,
            down.reshape(8, channels, wide), coarse)


def solution(mesh):
    both = ("region", "space")
    return jax.shard_map(
        on_device,
        mesh=mesh,
        in_specs=(P(both, None, None), P(), P(), P(), P(both, None, None), P(both, None),
                  P(both, None), P(both), P(both, None)),
        out_specs=(P(both, None, None), P(both, None, None), P(), P(), P()),
        check_vma=False,
    )
```

time: 81.4 us -> 64.6 us (0.79)
  Pallas kernels: 76.9 us -> 62.3 us
  local copies, waits for them, and re-layouts: 3.64 us -> 1.36 us
    pallas_call x1, Pallas kernels: 13.4 us -> 3.92 us  [on_device(): pl.pallas_call(result_kernel, out_shape=(shape((bricks, channels, volume)...]
    pallas_call x1, Pallas kernels: 62.1 us -> 55.6 us  [on_device(): pl.pallas_call(functools.partial(main_kernel, regions, owners, scale_fine...]
    slice x4 -> x0, local copies, waits for them, and re-layouts: 2.07 us -> none  [the longest x1 0.72 us: on_device(): totals[256:768].reshape(8, channels, wide)]
    pallas_call x1, Pallas kernels: 1.44 us -> 2.84 us  [on_device(): pl.pallas_call(index_kernel, out_shape=(shape((slots,), jnp.int32), shape...]
where the time goes in v2:
time: 64.6 us; the launch traced here: 64.4 us
  Pallas kernels  62.3 us (96%)
  local copies, waits for them, and re-layouts  1.36 us (2%)
  between operations  0.66 us (1%)
    pallas_call x1, Pallas kernels, on_device(): pl.pallas_call(functools.partial(main_kernel, regions, owners, scale_fine...  55.6 us
    pallas_call x1, Pallas kernels, on_device(): pl.pallas_call(result_kernel, out_shape=(shape((bricks, channels, volume)...  3.92 us
    pallas_call x1, Pallas kernels, on_device(): pl.pallas_call(index_kernel, out_shape=(shape((slots,), jnp.int32), shape...  2.84 us

profile of v2, /device:TPU:1, one launch (start us, length us, event | category | flops | bytes accessed | tf_op | source)
XLA Modules:
  0.0 64.4 jit_solution(12737365908239835802)
XLA Ops:
  0.6 0.0 copy-start
  0.6 0.7 %copy-done = s32[16,6]{0,1:T(8,128)S(1)} copy-done((s32[16,6]{0,1:T(8,128)S(1)}, s32[16,6]{0,1:T(8,128)}, u32[]{:S(2)}) %copy-start) | copy-done | bytes 408
  1.3 0.1 copy.18
  1.4 0.6 reshape.32.code_ref
  2.0 2.8 %index.1 = (s32[64]{0:T(128)}, s32[24]{0:T(128)}, s32[120]{0:T(128)}, s32[96]{0:T(128)}) custom-call(s32[96]{0:T(128)} %reshape.32.code_ref, s32[16]{0:T(128)} %slot_ref.3, s32[24]{0:T(128)} %bitcast.10), custom_call_target="tpu_custom_call" | custom-call | tf_op jit(solution)/shard_map/index/pallas_call | solution.py:687
  4.9 55.6 %main.1 = (bf16[16,64,512]{2,1,0:T(8,128)(2,1)}, bf16[64,64,128]{2,1,0:T(8,128)(2,1)}, f32[112,8,128]{2,1,0:T(8,128)}) custom-call(s32[96]{0:T(128)} %reshape.32.code_ref, s32[16]{0:T(128)} %slot_ref.3, s32[24]{0:T(128)} %bitcast.11, s32[64]{0:T(128)} %bitcast.8, s32[64]{0:T(128)} %get-tuple-element.17.child_inv, s32[24]{0:T(128)} %get-tuple-element.18.face_inv, ...), custom_call_target="tpu_custom_call" | custom-call | tf_op jit(solution)/shard_map/main/pallas_call | solution.py:704
  60.4 3.9 %result.1 = (bf16[16,64,512]{2,1,0:T(8,128)(2,1)}, bf16[64,64,128]{2,1,0:T(8,128)(2,1)}, f32[7,64,64]{2,1,0:T(8,128)}, f32[512,128]{1,0:T(8,128)}, f32[128,128]{1,0:T(8,128)}) custom-call(s32[64]{0:T(128)} %bitcast.9, bf16[16,64,512]{2,1,0:T(8,128)(2,1)} %get-tuple-element.21.made_ref, bf16[64,64,128]{2,1,0:T(8,128)(2,1)} %get-tuple-element.22.arr_ref, ...), custom_call_target="tpu_custom_call" | custom-call | tf_op jit(solution)/shard_map/result/pallas_call | solution.py:732
Async XLA Ops:
  0.6 0.7 %copy-start = (s32[16,6]{0,1:T(8,128)S(1)}, s32[16,6]{0,1:T(8,128)}, u32[]{:S(2)}) copy-start(s32[16,6]{0,1:T(8,128)} %param.17) | copy-start | bytes 1156

commit v3 on v2

--- a/solution.py
+++ b/solution.py
@@ -100,13 +100,13 @@
         device_id_type=MESH)
 
 
-def start_blocks(owners, my_r, my_s, pair, src, dst, send_sem, recv_sem):
+def start_blocks(owners, my_r, my_s, pair, first, end, src, dst, send_sem, recv_sem):
     def start(step, carry):
         peer = lax.rem(my_s + step, owners)
         block_copy(my_r, peer, pair, peer, my_s, src, dst, send_sem, recv_sem).start()
         return carry
 
-    lax.fori_loop(1, owners, start, 0)
+    lax.fori_loop(first, end, start, 0)
 
 
 def wait_blocks(owners, my_r, my_s, pair, src, dst, send_sem, recv_sem):
@@ -152,53 +152,6 @@
     return plan
 
 
-def index_kernel(code_ref, slot_ref, req_ref, child_ref, face_ref, prev_ref, last_ref):
-    total = code_ref.shape[0]
-    none = prev_ref.shape[0]
-    for s in range(child_ref.shape[0]):
-        child_ref[s] = 0
-    for s in range(face_ref.shape[0]):
-        face_ref[s] = 0
-    for f in range(total):
-        last_ref[f] = none
-    for b in range(slot_ref.shape[0]):
-        child_ref[slot_ref[b]] = b
-
-    def mark(n, carry):
-        code = code_ref[n]
-
-        @pl.when(code >= total)
-        def _():
-            face_ref[code - total] = n
-
-        @pl.when((code >= 0) & (code < total))
-        def _():
-            prev_ref[n] = last_ref[code]
-            last_ref[code] = n
-
-        @pl.when((code < 0) | (code >= total))
-        def _():
-            prev_ref[n] = none
-        return carry
-
-    lax.fori_loop(0, total, mark, 0)
-
-    def answer(s, carry):
-        want = req_ref[s]
-
-        @pl.when(want >= 0)
-        def _():
-            prev_ref[total + s] = last_ref[want]
-            last_ref[want] = total + s
-
-        @pl.when(want < 0)
-        def _():
-            prev_ref[total + s] = none
-        return carry
-
-    lax.fori_loop(0, req_ref.shape[0], answer, 0)
-
-
 def signal_peers(regions, owners, my_r, my_s):
     barrier = pltpu.get_barrier_semaphore()
 
@@ -228,7 +181,7 @@
 
 
 def main_kernel(regions, owners, scale_fine, scale_coarse,
-                code_ref, slot_ref, req_ref, po_ref, child_inv, face_inv, prev_ref, last_ref,
+                code_ref, slot_ref, req_ref, po_ref,
                 feat_hbm, cot_hbm, order_t_hbm, order_hbm, face_ref, fine_ref, down_ref,
                 coarse_ref,
                 grad_ref, blocks_out, total_ref,
@@ -236,8 +189,8 @@
                 got_cots, w_ref, wt_ref, taps_ref, act_ref, gh_ref, red_ref, cg_ref, ch_ref,
                 co_ref, co_slots, slope_ref, cslope_ref, gin_ref, plane_ref, back_face, ans_ref,
                 chain, halo_scr, g_scr,
-                grads, pair_got, half_sum, part_x, x_sum, part_p, mine,
-                load, fsend, frecv, hsend, hrecv, osem, bsem, csem, rsem):
+                grads, pair_got, half_sum, part_x, x_sum, part_p, mine, lists_v, lists,
+                load, lsem, fsend, frecv, hsend, hrecv, osem, bsem, csem, rsem):
     my_r = lax.axis_index("region")
     my_s = lax.axis_index("space")
     bricks = feat.shape[0]
@@ -259,6 +212,9 @@
         return carry
 
     lax.fori_loop(0, slots, gather_cot, 0, unroll=8)
+    wait_peers(regions, owners)
+    early = 1 + owners // 5
+    start_blocks(owners, my_r, my_s, pair, 1, early, cots, got_cots, bsem.at[0], bsem.at[1])
     loads[0].wait()
     loads[1].wait()
 
@@ -288,9 +244,48 @@
     lax.fori_loop(0, groups, turn, 0)
     for s in range(24):
         out_face[s // 4, s % 4] = table[jnp.maximum(req_ref[s], 0)]
-    wait_peers(regions, owners)
     send_faces(regions, owners, my_r, my_s, False, out_face, in_face, fsend, frecv)
-    start_blocks(owners, my_r, my_s, pair, cots, got_cots, bsem.at[0], bsem.at[1])
+    start_blocks(owners, my_r, my_s, pair, early, owners, cots, got_cots, bsem.at[0], bsem.at[1])
+
+    def code_of(n):
+        return code_ref[lax.rem(n, 6), n // 6]
+
+    none = face_total + 24
+    lanes = lax.broadcasted_iota(jnp.int32, (8, 128), 1)
+    child = jnp.zeros((8, 128), jnp.int32)
+    for b in range(bricks):
+        child = jnp.where(lanes == slot_ref[b], b, child)
+
+    def enter(n, target, carry):
+        targets, last = carry
+        return jnp.where(lanes == n, target, targets), jnp.where(lanes == target, n, last)
+
+    def own_entry(n, carry):
+        code = code_of(n)
+        plane = jnp.where(lanes == code - face_total, n, carry[0])
+        return (plane,) + enter(n, jnp.where(code < face_total, code, -1), carry[1:])
+
+    plane, targets, last = lax.fori_loop(
+        0, face_total, own_entry,
+        (jnp.zeros((8, 128), jnp.int32), jnp.full((8, 128), -2, jnp.int32),
+         jnp.full((8, 128), none, jnp.int32)), unroll=8)
+    for n in range(24):
+        targets, last = enter(face_total + n, req_ref[n], (targets, last))
+
+    def link(n, target, prev):
+        return jnp.where(targets == target, jnp.where(lanes > n, n, prev), prev)
+
+    def own_link(n, prev):
+        code = code_of(n)
+        return link(n, jnp.where(code < face_total, code, -1), prev)
+
+    prev = lax.fori_loop(0, face_total, own_link, jnp.full((8, 128), none, jnp.int32), unroll=8)
+    for n in range(24):
+        prev = link(face_total + n, req_ref[n], prev)
+    lists_v[...] = jnp.concatenate([child[0:1], plane[0:1], prev[0:1], last[0:1], child[0:4]], axis=0)
+    move = pltpu.make_async_copy(lists_v, lists, lsem)
+    move.start()
+    move.wait()
     plan = fill_weights(fine_ref, w_ref, wt_ref)
     wait_faces(regions, owners, my_r, my_s, False, out_face, in_face, fsend, frecv)
 
@@ -302,7 +297,7 @@
     low4 = lax.rem(lax.broadcasted_iota(jnp.int32, (32, 128), 0), 8) < 4
 
     def halo(b, d):
-        code = code_ref[b * 6 + d]
+        code = code_ref[d, b]
         own = table[jnp.clip(code, 0, face_total - 1)]
         slot = jnp.clip(code - face_total, 0, 23)
         got = in_face[slot // 4, lax.rem(slot, 4)]
@@ -327,8 +322,9 @@
         return jnp.where(low4, pieces8(values, 0, 32, 4),
                          row_roll(pieces8(values, 16, 32, 4), 4))
 
-    def forward_taps(b, n):
-        row = pl.multiple_of(b * ROWS, ROWS)
+    def forward_taps(g, n):
+        b = g * GROUP + n
+        row = pl.multiple_of(pl.multiple_of(g * wide_rows, wide_rows) + n * ROWS, ROWS)
         x = x_ref[pl.ds(row, ROWS), :]
         xk = xk_ref[pl.ds(row, ROWS), :].astype(F32)
         x32 = x.astype(F32)
@@ -352,11 +348,12 @@
             first_k, edge, row_roll(xk[:, 128:256], 1)).astype(BF)
 
     def forward(g, carry):
-        for n in range(GROUP):
-            forward_taps(g * GROUP + n, n)
         row = pl.multiple_of(g * wide_rows, wide_rows)
         half = pl.multiple_of(g * half_rows, half_rows)
+        forward_taps(g, 0)
         for n in range(GROUP):
+            if n + 1 < GROUP:
+                forward_taps(g, n + 1)
             part = pl.ds(pl.multiple_of(row + n * ROWS, ROWS), ROWS)
             hidden = dot(taps_ref[part, :], w_ref[...])
             act, slope = silu_parts(hidden)
@@ -378,14 +375,20 @@
     lax.fori_loop(0, groups, forward, 0)
 
     def gather_out(s, carry):
-        co_slots[s] = co_ref[child_inv[s]]
+        co_slots[s] = co_ref[lists[0, s]]
         return carry
 
     lax.fori_loop(0, slots, gather_out, 0, unroll=8)
     wait_blocks(owners, my_r, my_s, pair, cots, got_cots, bsem.at[0], bsem.at[1])
     for u in range(pair):
         got_cots[my_s * pair + u] = cots[my_s * pair + u]
-    start_blocks(owners, my_r, my_s, pair, co_slots, blocks_out, csem.at[0], csem.at[1])
+    cuts = (1, 1 + owners // 2, 1 + 3 * owners // 4, owners)
+
+    def send_out(n):
+        start_blocks(owners, my_r, my_s, pair, cuts[n], cuts[n + 1], co_slots, blocks_out,
+                     csem.at[0], csem.at[1])
+
+    send_out(0)
     keep = pltpu.make_async_copy(co_slots.at[pl.ds(my_s * pair, pair)],
                                  blocks_out.at[pl.ds(my_s * pair, pair)], osem)
     keep.start()
@@ -477,22 +480,23 @@
 
     for g in range(groups):
         backward(g)
-        if g == 0 or g == 2:
+        if g == 0:
             next(phases)
     for s in range(24):
-        back_face[s // 4, s % 4] = plane_ref[face_inv[s]]
+        back_face[s // 4, s % 4] = plane_ref[lists[1, s]]
     chain[face_total + 24] = jnp.zeros((32, 128), F32)
     send_faces(regions, owners, my_r, my_s, True, back_face, ans_ref, hsend, hrecv)
 
     def add_plane(n, carry):
-        chain[n] = chain[prev_ref[n]] + plane_ref[n].astype(F32)
+        chain[n] = chain[lists[2, n]] + plane_ref[n].astype(F32)
         return carry
 
     lax.fori_loop(0, face_total, add_plane, 0, unroll=4)
     next(phases)
+    send_out(1)
     wait_faces(regions, owners, my_r, my_s, True, back_face, ans_ref, hsend, hrecv)
     for s in range(24):
-        chain[face_total + s] = (chain[prev_ref[face_total + s]]
+        chain[face_total + s] = (chain[lists[2, face_total + s]]
                                  + ans_ref[s // 4, s % 4].astype(F32))
     loads[3].wait()
     lane = lax.broadcasted_iota(jnp.int32, (ROWS, LANES), 1)
@@ -503,7 +507,7 @@
         wides = []
         for n in range(GROUP):
             b = g * GROUP + n
-            f = [chain[last_ref[b * 6 + d]] for d in range(6)]
+            f = [chain[lists[3, b * 6 + d]] for d in range(6)]
             zero = jnp.zeros((ROWS, 128), F32)
             add_j = jnp.concatenate([jnp.where(first_j, spread_j(f[2], False), zero),
                                      jnp.where(last_j, spread_j(f[3], True), zero)], axis=1)
@@ -526,6 +530,8 @@
         return carry
 
     lax.fori_loop(0, groups, finish, 0)
+    next(phases)
+    send_out(2)
     for _ in phases:
         pass
     keep.wait()
@@ -592,7 +598,7 @@
 
     def wait_sent(count, n, src):
         if count:
-            remote(src.at[pl.ds(0, count * unit)], part_p.at[pl.ds(0, count * unit)], n,
+            remote(src.at[pl.ds(0, count * unit)], src.at[pl.ds(0, count * unit)], n,
                    near).wait_send()
 
     def wait_got(count, n, dst):
@@ -607,8 +613,8 @@
         run = x_sum[pl.ds(mine_at, unit)]
         for n in range(1, places):
             run = run + part_p[pl.ds(lax.rem(place_ + n, places) * unit, unit)]
-        mine[...] = run
-        total_ref[pl.ds(out_at, unit)] = run
+        mine[...] = run.astype(BF)
+        total_ref[pl.ds(out_at, unit)] = run.astype(BF)
 
         def start_share(n, carry):
             remote(mine, total_ref.at[pl.ds(out_at, unit)], 3,
@@ -624,7 +630,7 @@
 
     @pl.when(owns)
     def _():
-        wait_sent(places - 1, 3, part_p)
+        wait_sent(places - 1, 3, total_ref)
         wait_got(used - 1, 3, total_ref)
 
     @pl.when(jnp.logical_not(owns))
@@ -648,24 +654,35 @@
 
 
 def result_kernel(slot_ref, made_ref, arr_ref, total_ref, grad_ref, out_ref, fine_ref, down_ref,
-                  coarse_ref):
-    out_ref[...] = jnp.zeros_like(out_ref)
+                  coarse_ref, made, arrived, out, sem):
+    loads = [pltpu.make_async_copy(arr_ref, arrived, sem.at[0]),
+             pltpu.make_async_copy(made_ref, made, sem.at[1])]
+    for copy in loads:
+        copy.start()
+    out[...] = jnp.zeros_like(out)
+    for tap in range(7):
+        rows = total_ref[tap // 2 * 8:tap // 2 * 8 + 8].astype(F32).reshape(64, 128)
+        fine_ref[tap] = rows[:, tap % 2 * 64:tap % 2 * 64 + 64]
+    down_ref[...] = total_ref[32:96].astype(F32).reshape(512, 128)
+    coarse_ref[...] = total_ref[96:112].astype(F32).reshape(128, 128)
+    loads[0].wait()
 
     def put_block(s, carry):
         spot = slot_ref[s]
 
         @pl.when(spot >= 0)
         def _():
-            out_ref[spot] = arr_ref[s]
+            out[spot] = arrived[s]
         return carry
 
     lax.fori_loop(0, arr_ref.shape[0], put_block, 0, unroll=4)
-    grad_ref[...] = made_ref[...]
-    for tap in range(7):
-        rows = total_ref[tap // 2 * 8:tap // 2 * 8 + 8].reshape(64, 128)
-        fine_ref[tap] = rows[:, tap % 2 * 64:tap % 2 * 64 + 64]
-    down_ref[...] = total_ref[32:96].reshape(512, 128)
-    coarse_ref[...] = total_ref[96:112].reshape(128, 128)
+    stores = [pltpu.make_async_copy(out, out_ref, sem.at[2]),
+              pltpu.make_async_copy(made, grad_ref, sem.at[3])]
+    stores[0].start()
+    loads[1].wait()
+    stores[1].start()
+    for copy in stores:
+        copy.wait()
 
 
 def on_device(features, fine_weight, down_weight, coarse_weight, cotangent, face_source,
@@ -681,17 +698,8 @@
     shape = jax.ShapeDtypeStruct
     vm = pltpu.VMEM
     dma = pltpu.SemaphoreType.DMA
-    codes = face_source.reshape(faces)
     requests = face_requests.reshape(24)
     targets = parent_octant.reshape(slots)
-    child_inv, face_inv, prev, last = pl.pallas_call(
-        index_kernel,
-        out_shape=(shape((slots,), jnp.int32), shape((24,), jnp.int32),
-                   shape((faces + 24,), jnp.int32), shape((faces,), jnp.int32)),
-        in_specs=[SMEM_SPEC] * 3,
-        out_specs=(SMEM_SPEC,) * 4,
-        name="index",
-    )(codes, child_slot, requests)
     scale_fine = 1.0 / math.sqrt(bricks * count * volume)
     scale_coarse = 1.0 / math.sqrt(parents * count * volume)
     places = owners // 2
@@ -704,8 +712,8 @@
     made, arrived, totals = pl.pallas_call(
         functools.partial(main_kernel, regions, owners, scale_fine, scale_coarse),
         out_shape=(shape((bricks, channels, volume), BF), shape(block, BF),
-                   shape((112, 8, 128), F32)),
-        in_specs=[SMEM_SPEC] * 8 + [ANY_SPEC] * 4 + [VMEM_SPEC] * 4,
+                   shape((112, 8, 128), BF)),
+        in_specs=[SMEM_SPEC] * 4 + [ANY_SPEC] * 4 + [VMEM_SPEC] * 4,
         out_specs=(VMEM_SPEC, ANY_SPEC, VMEM_SPEC),
         scratch_shapes=[
             vm((bricks, channels, volume), BF), vm(block, BF), vm((512, 512), BF),
@@ -720,13 +728,13 @@
             vm((GROUP, ROWS, 128), F32), vm((2 * GROUP, ROWS, 128), F32),
             vm((112, 8, 128), F32), vm((56, 8, 128), F32), vm((56, 8, 128), F32),
             vm((56, 8, 128), F32), vm((per_r, 8, 128), F32), vm((places * unit, 8, 128), F32),
-            vm((unit, 8, 128), F32),
-            dma((4,)), dma((6,)), dma((6,)), dma((6,)), dma((6,)), dma, dma((2,)), dma((2,)),
+            vm((unit, 8, 128), BF), vm((8, 128), jnp.int32), pltpu.SMEM((8, 128), jnp.int32),
+            dma((4,)), dma, dma((6,)), dma((6,)), dma((6,)), dma((6,)), dma, dma((2,)), dma((2,)),
             dma((12,))],
         compiler_params=pltpu.CompilerParams(
             collective_id=0, has_side_effects=True, vmem_limit_bytes=60 * 2**20),
         name="main",
-    )(codes, child_slot, requests, targets, child_inv, face_inv, prev, last, features,
+    )(face_source.T, child_slot, requests, targets, features,
       cotangent.reshape(parents * 8, octant, wide), jnp.asarray(ORDER_T), jnp.asarray(ORDER),
       jnp.asarray(FACE), fine_weight, down_weight.reshape(8 * channels, wide), coarse_weight)
     grad_in, coarse_out, fine, down, coarse = pl.pallas_call(
@@ -734,8 +742,10 @@
         out_shape=(shape((bricks, channels, volume), BF), shape((parents * 8, octant, wide), BF),
                    shape((7, channels, channels), F32), shape((8 * channels, wide), F32),
                    shape((wide, wide), F32)),
-        in_specs=[SMEM_SPEC] + [VMEM_SPEC] * 3,
-        out_specs=(VMEM_SPEC,) * 5,
+        in_specs=[SMEM_SPEC, ANY_SPEC, ANY_SPEC, VMEM_SPEC],
+        out_specs=(ANY_SPEC,) * 2 + (VMEM_SPEC,) * 3,
+        scratch_shapes=[vm((bricks, channels, volume), BF), vm(block, BF),
+                        vm((parents * 8, octant, wide), BF), dma((4,))],
         compiler_params=pltpu.CompilerParams(vmem_limit_bytes=60 * 2**20),
         name="result",
     )(targets, made, arrived, totals)

time: 64.6 us -> 63.3 us (0.980)
  local copies, waits for them, and re-layouts: 1.36 us -> 0 us
    pallas_call x1 -> x0, Pallas kernels: 2.84 us -> none  [on_device(): pl.pallas_call(index_kernel, out_shape=(shape((slots,), jnp.int32), shape...]
    pallas_call x1, Pallas kernels: 55.6 us -> 57.8 us  [on_device(): pl.pallas_call(functools.partial(main_kernel, regions, owners, scale_fine...]
    unnamed x3 -> x0, local copies, waits for them, and re-layouts: 0.76 us -> none
    pallas_call x1, Pallas kernels: 3.92 us -> 4.64 us  [on_device(): pl.pallas_call(result_kernel, out_shape=(shape((bricks, channels, volume)...]
where the time goes in v3:
time: 63.3 us; the launch traced here: 63.1 us
  Pallas kernels  62.4 us (99%)
  between operations  0.64 us (1%)
    pallas_call x1, Pallas kernels, on_device(): pl.pallas_call(functools.partial(main_kernel, regions, owners, scale_fine...  57.8 us
    pallas_call x1, Pallas kernels, on_device(): pl.pallas_call(result_kernel, out_shape=(shape((bricks, channels, volume)...  4.64 us

profile of v3, /device:TPU:1, one launch (start us, length us, event | category | flops | bytes accessed | tf_op | source)
XLA Modules:
  0.0 63.1 jit_solution(3376092212089339468)
XLA Ops:
  0.6 57.8 %main.1 = (bf16[16,64,512]{2,1,0:T(8,128)(2,1)}, bf16[64,64,128]{2,1,0:T(8,128)(2,1)}, bf16[112,8,128]{2,1,0:T(8,128)(2,1)}) custom-call(s32[6,16]{1,0:T(8,128)} %bitcast.9, s32[16]{0:T(128)} %slot_ref.1, s32[24]{0:T(128)} %bitcast.12, s32[64]{0:T(128)} %bitcast.10, bf16[16,64,512]{2,1,0:T(8,128)(2,1)} %feat_hbm.1, bf16[64,64,128]{2,1,0:T(8,128)(2,1)} %bitcast.7, ...), custom_call_target="tpu_custom_call" | custom-call | tf_op jit(solution)/shard_map/main/pallas_call | solution.py:712
  58.4 4.6 %result.1 = (bf16[16,64,512]{2,1,0:T(8,128)(2,1)}, bf16[64,64,128]{2,1,0:T(8,128)(2,1)}, f32[7,64,64]{2,1,0:T(8,128)}, f32[512,128]{1,0:T(8,128)}, f32[128,128]{1,0:T(8,128)}) custom-call(s32[64]{0:T(128)} %bitcast.11, bf16[16,64,512]{2,1,0:T(8,128)(2,1)} %get-tuple-element.13.made_ref, bf16[64,64,128]{2,1,0:T(8,128)(2,1)} %get-tuple-element.14.arr_ref, ...), custom_call_target="tpu_custom_call" | custom-call | tf_op jit(solution)/shard_map/result/pallas_call | solution.py:740

commit v4 on v3

--- a/solution.py
+++ b/solution.py
@@ -100,13 +100,21 @@
         device_id_type=MESH)
 
 
+def peer_order(owners):
+    rows = owners // 8
+    if rows < 4:
+        return [(0, n // 2, n % 2) for n in range(1, owners)]
+    far = [(2, 2), (2, 1), (1, 2), (2, 3), (3, 2), (1, 1), (3, 3), (1, 3), (3, 1), (2, 0), (0, 2),
+           (1, 0), (0, 3), (3, 0), (0, 1)]
+    return [(a, b, c) for a, b in far for c in (0, 1)] + [(0, 0, 1)]
+
+
 def start_blocks(owners, my_r, my_s, pair, first, end, src, dst, send_sem, recv_sem):
-    def start(step, carry):
-        peer = lax.rem(my_s + step, owners)
+    rows, line = max(1, owners // 8), min(4, owners // 2)
+    z, y, core = my_s // (2 * line), lax.rem(my_s // 2, line), lax.rem(my_s, 2)
+    for dz, dy, dc in peer_order(owners)[first:end]:
+        peer = (lax.rem(z + dz, rows) * line + lax.rem(y + dy, line)) * 2 + lax.rem(core + dc, 2)
         block_copy(my_r, peer, pair, peer, my_s, src, dst, send_sem, recv_sem).start()
-        return carry
-
-    lax.fori_loop(first, end, start, 0)
 
 
 def wait_blocks(owners, my_r, my_s, pair, src, dst, send_sem, recv_sem):
@@ -162,14 +170,21 @@
 
     lax.fori_loop(1, owners, greet, 0)
 
-    for step in range(1, regions):
-        far_r = lax.rem(my_r + step, regions)
-        pl.semaphore_signal(barrier, inc=1, device_id=(far_r, my_s), device_id_type=MESH)
+    core = lax.rem(my_s, 2)
+
+    def greet_far(place_, carry):
+        for step in range(1, regions):
+            far_r = lax.rem(my_r + step, regions)
+            pl.semaphore_signal(barrier, inc=1, device_id=(far_r, 2 * place_ + core),
+                                device_id_type=MESH)
+        return carry
+
+    lax.fori_loop(0, owners // 2, greet_far, 0)
 
 
 def wait_peers(regions, owners):
     barrier = pltpu.get_barrier_semaphore()
-    pl.semaphore_wait(barrier, owners - 1 + regions - 1)
+    pl.semaphore_wait(barrier, owners - 1 + (regions - 1) * (owners // 2))
 
 
 def row_roll(v, by):
@@ -189,7 +204,7 @@
                 got_cots, w_ref, wt_ref, taps_ref, act_ref, gh_ref, red_ref, cg_ref, ch_ref,
                 co_ref, co_slots, slope_ref, cslope_ref, gin_ref, plane_ref, back_face, ans_ref,
                 chain, halo_scr, g_scr,
-                grads, pair_got, half_sum, part_x, x_sum, part_p, mine, lists_v, lists,
+                grads, pair_got, half_sum, part_p, mine, lists_v, lists,
                 load, lsem, fsend, frecv, hsend, hrecv, osem, bsem, csem, rsem):
     my_r = lax.axis_index("region")
     my_s = lax.axis_index("space")
@@ -213,8 +228,8 @@
 
     lax.fori_loop(0, slots, gather_cot, 0, unroll=8)
     wait_peers(regions, owners)
-    early = 1 + owners // 5
-    start_blocks(owners, my_r, my_s, pair, 1, early, cots, got_cots, bsem.at[0], bsem.at[1])
+    early = owners // 5
+    start_blocks(owners, my_r, my_s, pair, 0, early, cots, got_cots, bsem.at[0], bsem.at[1])
     loads[0].wait()
     loads[1].wait()
 
@@ -245,10 +260,7 @@
     for s in range(24):
         out_face[s // 4, s % 4] = table[jnp.maximum(req_ref[s], 0)]
     send_faces(regions, owners, my_r, my_s, False, out_face, in_face, fsend, frecv)
-    start_blocks(owners, my_r, my_s, pair, early, owners, cots, got_cots, bsem.at[0], bsem.at[1])
-
-    def code_of(n):
-        return code_ref[lax.rem(n, 6), n // 6]
+    start_blocks(owners, my_r, my_s, pair, early, owners - 1, cots, got_cots, bsem.at[0], bsem.at[1])
 
     none = face_total + 24
     lanes = lax.broadcasted_iota(jnp.int32, (8, 128), 1)
@@ -260,26 +272,31 @@
         targets, last = carry
         return jnp.where(lanes == n, target, targets), jnp.where(lanes == target, n, last)
 
-    def own_entry(n, carry):
-        code = code_of(n)
-        plane = jnp.where(lanes == code - face_total, n, carry[0])
-        return (plane,) + enter(n, jnp.where(code < face_total, code, -1), carry[1:])
+    def own_entry(b, carry):
+        plane, state = carry[0], carry[1:]
+        for d in range(6):
+            code = code_ref[d, b]
+            plane = jnp.where(lanes == code - face_total, b * 6 + d, plane)
+            state = enter(b * 6 + d, jnp.where(code < face_total, code, -1), state)
+        return (plane,) + state
 
     plane, targets, last = lax.fori_loop(
-        0, face_total, own_entry,
+        0, bricks, own_entry,
         (jnp.zeros((8, 128), jnp.int32), jnp.full((8, 128), -2, jnp.int32),
-         jnp.full((8, 128), none, jnp.int32)), unroll=8)
+         jnp.full((8, 128), none, jnp.int32)), unroll=2)
     for n in range(24):
         targets, last = enter(face_total + n, req_ref[n], (targets, last))
 
     def link(n, target, prev):
         return jnp.where(targets == target, jnp.where(lanes > n, n, prev), prev)
 
-    def own_link(n, prev):
-        code = code_of(n)
-        return link(n, jnp.where(code < face_total, code, -1), prev)
-
-    prev = lax.fori_loop(0, face_total, own_link, jnp.full((8, 128), none, jnp.int32), unroll=8)
+    def own_link(b, prev):
+        for d in range(6):
+            code = code_ref[d, b]
+            prev = link(b * 6 + d, jnp.where(code < face_total, code, -1), prev)
+        return prev
+
+    prev = lax.fori_loop(0, bricks, own_link, jnp.full((8, 128), none, jnp.int32), unroll=2)
     for n in range(24):
         prev = link(face_total + n, req_ref[n], prev)
     lists_v[...] = jnp.concatenate([child[0:1], plane[0:1], prev[0:1], last[0:1], child[0:4]], axis=0)
@@ -382,7 +399,7 @@
     wait_blocks(owners, my_r, my_s, pair, cots, got_cots, bsem.at[0], bsem.at[1])
     for u in range(pair):
         got_cots[my_s * pair + u] = cots[my_s * pair + u]
-    cuts = (1, 1 + owners // 2, 1 + 3 * owners // 4, owners)
+    cuts = (0, owners // 2, owners - 1)
 
     def send_out(n):
         start_blocks(owners, my_r, my_s, pair, cuts[n], cuts[n + 1], co_slots, blocks_out,
@@ -429,8 +446,8 @@
         put_rows(n * 64, jnp.concatenate([sums[2 * n], sums[2 * n + 1]], axis=0).T)
     put_rows(256, dot(act_ref[...], ch_ref[...], TN) * scale_fine)
     put_rows(768, dot(red_ref[...], cg_ref[...], TN) * scale_coarse)
-    phases = sum_phases(regions, owners, my_r, my_s, grads, pair_got, half_sum, part_x, x_sum,
-                        part_p, mine, total_ref, rsem)
+    phases = sum_phases(regions, owners, my_r, my_s, grads, pair_got, half_sum, part_p, mine,
+                        total_ref, rsem)
     next(phases)
 
     def backward(g):
@@ -482,6 +499,7 @@
         backward(g)
         if g == 0:
             next(phases)
+            send_out(1)
     for s in range(24):
         back_face[s // 4, s % 4] = plane_ref[lists[1, s]]
     chain[face_total + 24] = jnp.zeros((32, 128), F32)
@@ -493,7 +511,6 @@
 
     lax.fori_loop(0, face_total, add_plane, 0, unroll=4)
     next(phases)
-    send_out(1)
     wait_faces(regions, owners, my_r, my_s, True, back_face, ans_ref, hsend, hrecv)
     for s in range(24):
         chain[face_total + s] = (chain[lists[2, face_total + s]]
@@ -530,159 +547,119 @@
         return carry
 
     lax.fori_loop(0, groups, finish, 0)
-    next(phases)
-    send_out(2)
     for _ in phases:
         pass
     keep.wait()
     wait_blocks(owners, my_r, my_s, pair, co_slots, blocks_out, csem.at[0], csem.at[1])
 
 
-def sum_phases(regions, owners, my_r, my_s, grads, pair_got, half_sum, part_x, x_sum, part_p, mine,
-               total_ref, sem):
+def sum_phases(regions, owners, my_r, my_s, grads, pair_got, half_sum, part_p, mine, total_ref, sem):
     core = lax.rem(my_s, 2)
     other = 1 - core
-    place_ = my_s // 2
-    places = owners // 2
+    width = owners // 2
+    chips = regions * width
+    chip = my_r * width + my_s // 2
     half = pair_got.shape[0]
-    per_r = half // regions
     unit = mine.shape[0]
-    used = per_r // unit
+    used = half // unit
     partner = (my_r, my_s + 1 - 2 * core)
 
     def remote(src, dst, n, target):
         return pltpu.make_async_remote_copy(
             src_ref=src, dst_ref=dst, send_sem=sem.at[2 * n], recv_sem=sem.at[2 * n + 1],
             device_id=target, device_id_type=MESH)
+
+    def spot(peer):
+        return (peer // width, 2 * lax.rem(peer, width) + core)
+
+    near = spot(lax.rem(chip + 1, chips))
+
+    def sized(ref, count, n):
+        part = ref.at[pl.ds(0, count * unit)]
+        return remote(part, part, n, near)
 
     swap = remote(grads.at[pl.ds(other * half, half)], pair_got, 0, partner)
     swap.start()
     yield
     swap.wait()
     half_sum[...] = grads[pl.ds(core * half, half)] + pair_got[...]
-    for n in range(1, regions):
-        peer = lax.rem(my_r + n, regions)
-        remote(half_sum.at[pl.ds(peer * per_r, per_r)], part_x.at[pl.ds(my_r * per_r, per_r)], 1,
-               (peer, my_s)).start()
-    yield
-    far = (lax.rem(my_r + 1, regions), my_s)
-    got = pl.ds(0, (regions - 1) * per_r)
-    arrived = remote(half_sum.at[got], part_x.at[got], 1, far)
-    arrived.wait_send()
-    arrived.wait_recv()
-    run = half_sum[pl.ds(my_r * per_r, per_r)]
-    for n in range(1, regions):
-        run = run + part_x[pl.ds(lax.rem(my_r + n, regions) * per_r, per_r)]
-    x_sum[...] = run
-
-    def spot(peer):
-        return (my_r, 2 * peer + core)
-
-    owns = place_ < used
-    mine_at = jnp.minimum(place_, used - 1) * unit
+    owns = chip < used
+    mine_at = jnp.minimum(chip, used - 1) * unit
 
     def start_sum(n, carry):
-        peer = lax.rem(place_ + n, places)
+        peer = lax.rem(chip + n, chips)
 
         @pl.when(peer < used)
         def _():
-            remote(x_sum.at[pl.ds(jnp.minimum(peer, used - 1) * unit, unit)],
-                   part_p.at[pl.ds(place_ * unit, unit)], 2, spot(peer)).start()
-        return carry
-
-    lax.fori_loop(1, places, start_sum, 0)
+            remote(half_sum.at[pl.ds(jnp.minimum(peer, used - 1) * unit, unit)],
+                   part_p.at[pl.ds(chip * unit, unit)], 1, spot(peer)).start()
+        return carry
+
+    lax.fori_loop(1, chips, start_sum, 0)
     yield
-    near = spot(lax.rem(place_ + 1, places))
-    base = core * half + my_r * per_r
-    out_at = base + mine_at
-
-    def wait_sent(count, n, src):
-        if count:
-            remote(src.at[pl.ds(0, count * unit)], src.at[pl.ds(0, count * unit)], n,
-                   near).wait_send()
-
-    def wait_got(count, n, dst):
-        if count:
-            remote(dst.at[pl.ds(0, count * unit)], dst.at[pl.ds(0, count * unit)], n,
-                   near).wait_recv()
+    out_at = core * half + mine_at
 
     @pl.when(owns)
     def _():
-        wait_sent(used - 1, 2, x_sum)
-        wait_got(places - 1, 2, part_p)
-        run = x_sum[pl.ds(mine_at, unit)]
-        for n in range(1, places):
-            run = run + part_p[pl.ds(lax.rem(place_ + n, places) * unit, unit)]
+        sized(half_sum, used - 1, 1).wait_send()
+        sized(part_p, chips - 1, 1).wait_recv()
+        part_p[pl.ds(chip * unit, unit)] = half_sum[pl.ds(mine_at, unit)]
+        run = part_p[0:unit]
+        for n in range(1, chips):
+            run = run + part_p[n * unit:n * unit + unit]
         mine[...] = run.astype(BF)
         total_ref[pl.ds(out_at, unit)] = run.astype(BF)
 
         def start_share(n, carry):
-            remote(mine, total_ref.at[pl.ds(out_at, unit)], 3,
-                   spot(lax.rem(place_ + n, places))).start()
+            remote(mine, total_ref.at[pl.ds(out_at, unit)], 2,
+                   spot(lax.rem(chip + n, chips))).start()
             return carry
 
-        lax.fori_loop(1, places, start_share, 0)
-
-    @pl.when(jnp.logical_not(owns))
-    def _():
-        wait_sent(used, 2, x_sum)
+        lax.fori_loop(1, chips, start_share, 0)
+
+    if used < chips:
+        @pl.when(jnp.logical_not(owns))
+        def _():
+            sized(half_sum, used, 1).wait_send()
     yield
 
     @pl.when(owns)
     def _():
-        wait_sent(places - 1, 3, total_ref)
-        wait_got(used - 1, 3, total_ref)
-
-    @pl.when(jnp.logical_not(owns))
-    def _():
-        wait_got(used, 3, total_ref)
-
-    for n in range(1, regions):
-        peer = lax.rem(my_r + n, regions)
-        remote(total_ref.at[pl.ds(base, per_r)], total_ref.at[pl.ds(base, per_r)], 4,
-               (peer, my_s)).start()
+        sized(total_ref, chips - 1, 2).wait_send()
+        sized(total_ref, used - 1, 2).wait_recv()
+
+    if used < chips:
+        @pl.when(jnp.logical_not(owns))
+        def _():
+            sized(total_ref, used, 2).wait_recv()
+
+    own = pl.ds(core * half, half)
+    remote(total_ref.at[own], total_ref.at[own], 3, partner).start()
     yield
-    gone = remote(total_ref.at[got], total_ref.at[got], 4, far)
-    gone.wait_send()
-    gone.wait_recv()
-    own = pl.ds(core * half, half)
-    remote(total_ref.at[own], total_ref.at[own], 5, partner).start()
-    yield
-    last = remote(total_ref.at[own], total_ref.at[pl.ds(other * half, half)], 5, partner)
+    last = remote(total_ref.at[own], total_ref.at[pl.ds(other * half, half)], 3, partner)
     last.wait_send()
     last.wait_recv()
 
 
 def result_kernel(slot_ref, made_ref, arr_ref, total_ref, grad_ref, out_ref, fine_ref, down_ref,
-                  coarse_ref, made, arrived, out, sem):
-    loads = [pltpu.make_async_copy(arr_ref, arrived, sem.at[0]),
-             pltpu.make_async_copy(made_ref, made, sem.at[1])]
-    for copy in loads:
-        copy.start()
-    out[...] = jnp.zeros_like(out)
+                  coarse_ref):
+    out_ref[...] = jnp.zeros_like(out_ref)
+
+    def put_block(s, carry):
+        spot = slot_ref[s]
+
+        @pl.when(spot >= 0)
+        def _():
+            out_ref[spot] = arr_ref[s]
+        return carry
+
+    lax.fori_loop(0, arr_ref.shape[0], put_block, 0, unroll=4)
+    grad_ref[...] = made_ref[...]
     for tap in range(7):
         rows = total_ref[tap // 2 * 8:tap // 2 * 8 + 8].astype(F32).reshape(64, 128)
         fine_ref[tap] = rows[:, tap % 2 * 64:tap % 2 * 64 + 64]
     down_ref[...] = total_ref[32:96].astype(F32).reshape(512, 128)
     coarse_ref[...] = total_ref[96:112].astype(F32).reshape(128, 128)
-    loads[0].wait()
-
-    def put_block(s, carry):
-        spot = slot_ref[s]
-
-        @pl.when(spot >= 0)
-        def _():
-            out[spot] = arrived[s]
-        return carry
-
-    lax.fori_loop(0, arr_ref.shape[0], put_block, 0, unroll=4)
-    stores = [pltpu.make_async_copy(out, out_ref, sem.at[2]),
-              pltpu.make_async_copy(made, grad_ref, sem.at[3])]
-    stores[0].start()
-    loads[1].wait()
-    stores[1].start()
-    for copy in stores:
-        copy.wait()
 
 
 def on_device(features, fine_weight, down_weight, coarse_weight, cotangent, face_source,
@@ -702,9 +679,8 @@
     targets = parent_octant.reshape(slots)
     scale_fine = 1.0 / math.sqrt(bricks * count * volume)
     scale_coarse = 1.0 / math.sqrt(parents * count * volume)
-    places = owners // 2
-    per_r = 56 // regions
-    unit = max(1, per_r // places)
+    chips = count // 2
+    unit = max(1, 56 // chips)
     big = bricks * ROWS
     small = bricks * octant
     block = (slots, octant, wide)
@@ -727,10 +703,10 @@
             vm(faces4, BF), vm(faces4, BF), vm((faces + 25, 32, 128), F32),
             vm((GROUP, ROWS, 128), F32), vm((2 * GROUP, ROWS, 128), F32),
             vm((112, 8, 128), F32), vm((56, 8, 128), F32), vm((56, 8, 128), F32),
-            vm((56, 8, 128), F32), vm((per_r, 8, 128), F32), vm((places * unit, 8, 128), F32),
+            vm((chips * unit, 8, 128), F32),
             vm((unit, 8, 128), BF), vm((8, 128), jnp.int32), pltpu.SMEM((8, 128), jnp.int32),
             dma((4,)), dma, dma((6,)), dma((6,)), dma((6,)), dma((6,)), dma, dma((2,)), dma((2,)),
-            dma((12,))],
+            dma((8,))],
         compiler_params=pltpu.CompilerParams(
             collective_id=0, has_side_effects=True, vmem_limit_bytes=60 * 2**20),
         name="main",
@@ -742,10 +718,8 @@
         out_shape=(shape((bricks, channels, volume), BF), shape((parents * 8, octant, wide), BF),
                    shape((7, channels, channels), F32), shape((8 * channels, wide), F32),
                    shape((wide, wide), F32)),
-        in_specs=[SMEM_SPEC, ANY_SPEC, ANY_SPEC, VMEM_SPEC],
-        out_specs=(ANY_SPEC,) * 2 + (VMEM_SPEC,) * 3,
-        scratch_shapes=[vm((bricks, channels, volume), BF), vm(block, BF),
-                        vm((parents * 8, octant, wide), BF), dma((4,))],
+        in_specs=[SMEM_SPEC] + [VMEM_SPEC] * 3,
+        out_specs=(VMEM_SPEC,) * 5,
         compiler_params=pltpu.CompilerParams(vmem_limit_bytes=60 * 2**20),
         name="result",
     )(targets, made, arrived, totals)

time: 63.3 us -> 58 us (0.916)
  Pallas kernels: 62.4 us -> 57.1 us
    pallas_call x1, Pallas kernels: 57.8 us -> 53.3 us  [on_device(): pl.pallas_call(functools.partial(main_kernel, regions, owners, scale_fine...]
    pallas_call x1, Pallas kernels: 4.64 us -> 3.85 us  [on_device(): pl.pallas_call(result_kernel, out_shape=(shape((bricks, channels, volume)...]
where the time goes in v4:
time: 58 us; the launch traced here: 57.8 us
  Pallas kernels  57.1 us (98%)
  between operations  0.64 us (1%)
    pallas_call x1, Pallas kernels, on_device(): pl.pallas_call(functools.partial(main_kernel, regions, owners, scale_fine...  53.3 us
    pallas_call x1, Pallas kernels, on_device(): pl.pallas_call(result_kernel, out_shape=(shape((bricks, channels, volume)...  3.85 us

profile of v4, /device:TPU:1, one launch (start us, length us, event | category | flops | bytes accessed | tf_op | source)
XLA Modules:
  0.0 57.8 jit_solution(2911506584147636341)
XLA Ops:
  0.6 53.3 %main.1 = (bf16[16,64,512]{2,1,0:T(8,128)(2,1)}, bf16[64,64,128]{2,1,0:T(8,128)(2,1)}, bf16[112,8,128]{2,1,0:T(8,128)(2,1)}) custom-call(s32[6,16]{1,0:T(8,128)} %bitcast.9, s32[16]{0:T(128)} %slot_ref.1, s32[24]{0:T(128)} %bitcast.12, s32[64]{0:T(128)} %bitcast.10, bf16[16,64,512]{2,1,0:T(8,128)(2,1)} %feat_hbm.1, bf16[64,64,128]{2,1,0:T(8,128)(2,1)} %bitcast.7, ...), custom_call_target="tpu_custom_call" | custom-call | tf_op jit(solution)/shard_map/main/pallas_call | solution.py:688
  53.9 3.8 %result.1 = (bf16[16,64,512]{2,1,0:T(8,128)(2,1)}, bf16[64,64,128]{2,1,0:T(8,128)(2,1)}, f32[7,64,64]{2,1,0:T(8,128)}, f32[512,128]{1,0:T(8,128)}, f32[128,128]{1,0:T(8,128)}) custom-call(s32[64]{0:T(128)} %bitcast.11, bf16[16,64,512]{2,1,0:T(8,128)(2,1)} %get-tuple-element.13.made_ref, bf16[64,64,128]{2,1,0:T(8,128)(2,1)} %get-tuple-element.14.arr_ref, ...), custom_call_target="tpu_custom_call" | custom-call | tf_op jit(solution)/shard_map/result/pallas_call | solution.py:716

commit v5 on v4

--- a/solution.py
+++ b/solution.py
@@ -220,19 +220,6 @@
     for copy in loads:
         copy.start()
     signal_peers(regions, owners, my_r, my_s)
-    loads[2].wait()
-
-    def gather_cot(s, carry):
-        cots[s] = cot[jnp.maximum(po_ref[s], 0)]
-        return carry
-
-    lax.fori_loop(0, slots, gather_cot, 0, unroll=8)
-    wait_peers(regions, owners)
-    early = owners // 5
-    start_blocks(owners, my_r, my_s, pair, 0, early, cots, got_cots, bsem.at[0], bsem.at[1])
-    loads[0].wait()
-    loads[1].wait()
-
     def turn(g, carry):
         block = feat[pl.ds(g * GROUP, GROUP)].reshape(half_rows, 512)
         moved = dot(block, order_t[...]).astype(BF)
@@ -256,7 +243,19 @@
             table[base + 5] = fk[32:64, 128:256]
         return carry
 
-    lax.fori_loop(0, groups, turn, 0)
+    def gather_cot(s, carry):
+        cots[s] = cot[jnp.maximum(po_ref[s], 0)]
+        return carry
+
+    loads[0].wait()
+    loads[1].wait()
+    lax.fori_loop(0, groups // 2, turn, 0)
+    loads[2].wait()
+    lax.fori_loop(0, slots, gather_cot, 0, unroll=8)
+    wait_peers(regions, owners)
+    early = owners // 8
+    start_blocks(owners, my_r, my_s, pair, 0, early, cots, got_cots, bsem.at[0], bsem.at[1])
+    lax.fori_loop(groups // 2, groups, turn, 0)
     for s in range(24):
         out_face[s // 4, s % 4] = table[jnp.maximum(req_ref[s], 0)]
     send_faces(regions, owners, my_r, my_s, False, out_face, in_face, fsend, frecv)
@@ -543,12 +542,15 @@
             flipped = total.T
             wides.append(jnp.concatenate([flipped[q * 64:q * 64 + 64] for q in range(4)], axis=1))
         out = dot(jnp.concatenate(wides, axis=0), order[...]).astype(BF)
-        grad_ref[pl.ds(g * GROUP, GROUP)] = out.reshape(GROUP, 64, 512)
+        feat[pl.ds(g * GROUP, GROUP)] = out.reshape(GROUP, 64, 512)
         return carry
 
     lax.fori_loop(0, groups, finish, 0)
+    leave = pltpu.make_async_copy(feat, grad_ref, lsem)
+    leave.start()
     for _ in phases:
         pass
+    leave.wait()
     keep.wait()
     wait_blocks(owners, my_r, my_s, pair, co_slots, blocks_out, csem.at[0], csem.at[1])
 
@@ -690,7 +692,7 @@
         out_shape=(shape((bricks, channels, volume), BF), shape(block, BF),
                    shape((112, 8, 128), BF)),
         in_specs=[SMEM_SPEC] * 4 + [ANY_SPEC] * 4 + [VMEM_SPEC] * 4,
-        out_specs=(VMEM_SPEC, ANY_SPEC, VMEM_SPEC),
+        out_specs=(ANY_SPEC, ANY_SPEC, VMEM_SPEC),
         scratch_shapes=[
             vm((bricks, channels, volume), BF), vm(block, BF), vm((512, 512), BF),
             vm((512, 512), BF), vm((big, LANES), BF), vm((big, LANES), BF),

time: 58 us -> 57.5 us (level)
  no operation moved by 1% of the time
where the time goes in v5:
time: 57.5 us; the launch traced here: 57.4 us
  Pallas kernels  56.7 us (99%)
  between operations  0.64 us (1%)
    pallas_call x1, Pallas kernels, on_device(): pl.pallas_call(functools.partial(main_kernel, regions, owners, scale_fine...  52.9 us
    pallas_call x1, Pallas kernels, on_device(): pl.pallas_call(result_kernel, out_shape=(shape((bricks, channels, volume)...  3.84 us

profile of v5, /device:TPU:1, one launch (start us, length us, event | category | flops | bytes accessed | tf_op | source)
XLA Modules:
  0.0 57.4 jit_solution(5310376250964026723)
XLA Ops:
  0.6 52.9 %main.1 = (bf16[16,64,512]{2,1,0:T(8,128)(2,1)}, bf16[64,64,128]{2,1,0:T(8,128)(2,1)}, bf16[112,8,128]{2,1,0:T(8,128)(2,1)}) custom-call(s32[6,16]{1,0:T(8,128)} %bitcast.9, s32[16]{0:T(128)} %slot_ref.1, s32[24]{0:T(128)} %bitcast.12, s32[64]{0:T(128)} %bitcast.10, bf16[16,64,512]{2,1,0:T(8,128)(2,1)} %feat_hbm.1, bf16[64,64,128]{2,1,0:T(8,128)(2,1)} %bitcast.7, ...), custom_call_target="tpu_custom_call" | custom-call | tf_op jit(solution)/shard_map/main/pallas_call | solution.py:690
  53.5 3.8 %result.1 = (bf16[16,64,512]{2,1,0:T(8,128)(2,1)}, bf16[64,64,128]{2,1,0:T(8,128)(2,1)}, f32[7,64,64]{2,1,0:T(8,128)}, f32[512,128]{1,0:T(8,128)}, f32[128,128]{1,0:T(8,128)}) custom-call(s32[64]{0:T(128)} %bitcast.11, bf16[16,64,512]{2,1,0:T(8,128)(2,1)} %get-tuple-element.13.made_ref, bf16[64,64,128]{2,1,0:T(8,128)(2,1)} %get-tuple-element.14.arr_ref, ...), custom_call_target="tpu_custom_call" | custom-call | tf_op jit(solution)/shard_map/result/pallas_call | solution.py:718

commit v6 on v5

--- a/solution.py
+++ b/solution.py
@@ -398,7 +398,7 @@
     wait_blocks(owners, my_r, my_s, pair, cots, got_cots, bsem.at[0], bsem.at[1])
     for u in range(pair):
         got_cots[my_s * pair + u] = cots[my_s * pair + u]
-    cuts = (0, owners // 2, owners - 1)
+    cuts = (0, owners // 4, 7 * owners // 16, owners - 1)
 
     def send_out(n):
         start_blocks(owners, my_r, my_s, pair, cuts[n], cuts[n + 1], co_slots, blocks_out,
@@ -510,6 +510,7 @@
 
     lax.fori_loop(0, face_total, add_plane, 0, unroll=4)
     next(phases)
+    send_out(2)
     wait_faces(regions, owners, my_r, my_s, True, back_face, ans_ref, hsend, hrecv)
     for s in range(24):
         chain[face_total + s] = (chain[lists[2, face_total + s]]

time: 57.5 us -> 56.4 us (0.981)
  Pallas kernels: 56.7 us -> 55.6 us
    pallas_call x1, Pallas kernels: 52.9 us -> 51.8 us  [on_device(): pl.pallas_call(functools.partial(main_kernel, regions, owners, scale_fine...]
where the time goes in v6:
time: 56.4 us; the launch traced here: 56.3 us
  Pallas kernels  55.6 us (99%)
  between operations  0.64 us (1%)
    pallas_call x1, Pallas kernels, on_device(): pl.pallas_call(functools.partial(main_kernel, regions, owners, scale_fine...  51.8 us
    pallas_call x1, Pallas kernels, on_device(): pl.pallas_call(result_kernel, out_shape=(shape((bricks, channels, volume)...  3.84 us

profile of v6, /device:TPU:1, one launch (start us, length us, event | category | flops | bytes accessed | tf_op | source)
XLA Modules:
  0.0 56.3 jit_solution(1637717248379266475)
XLA Ops:
  0.6 51.8 %main.1 = (bf16[16,64,512]{2,1,0:T(8,128)(2,1)}, bf16[64,64,128]{2,1,0:T(8,128)(2,1)}, bf16[112,8,128]{2,1,0:T(8,128)(2,1)}) custom-call(s32[6,16]{1,0:T(8,128)} %bitcast.9, s32[16]{0:T(128)} %slot_ref.1, s32[24]{0:T(128)} %bitcast.12, s32[64]{0:T(128)} %bitcast.10, bf16[16,64,512]{2,1,0:T(8,128)(2,1)} %feat_hbm.1, bf16[64,64,128]{2,1,0:T(8,128)(2,1)} %bitcast.7, ...), custom_call_target="tpu_custom_call" | custom-call | tf_op jit(solution)/shard_map/main/pallas_call | solution.py:691
  52.4 3.8 %result.1 = (bf16[16,64,512]{2,1,0:T(8,128)(2,1)}, bf16[64,64,128]{2,1,0:T(8,128)(2,1)}, f32[7,64,64]{2,1,0:T(8,128)}, f32[512,128]{1,0:T(8,128)}, f32[128,128]{1,0:T(8,128)}) custom-call(s32[64]{0:T(128)} %bitcast.11, bf16[16,64,512]{2,1,0:T(8,128)(2,1)} %get-tuple-element.13.made_ref, bf16[64,64,128]{2,1,0:T(8,128)(2,1)} %get-tuple-element.14.arr_ref, ...), custom_call_target="tpu_custom_call" | custom-call | tf_op jit(solution)/shard_map/result/pallas_call | solution.py:719
